TPU v7x, 256 devices: a whole 4x4x8 slice. The times are simulated.
256 devices in a mesh: rep: 2 (over y_lo), exp: 128 (over y_hi, z, x, core).
Axes of the slice: x: 4, y: 4 (y_hi: 2, y_lo: 2; y = y_hi * 2 + y_lo), z: 8, core: 2. Of those that a mesh axis runs over, the one named last changes fastest.
Arguments:
- tokens: bfloat16 [32768, 2048], P(('rep', 'exp')), may hold values from -6 to 6
- out_grad: bfloat16 [32768, 2048], P(('rep', 'exp')), may hold values from -1.5 to 1.5
- route: int32 [32768, 4], P(('rep', 'exp')), may hold values from 0 to 127, as said below
- prob: bfloat16 [32768, 4], P(('rep', 'exp')), may hold values from 0.049804688 to 0.59765625
- w_gate: bfloat16 [128, 2048, 384], P('exp'), may hold values from -0.125 to 0.125
- w_up: bfloat16 [128, 2048, 384], P('exp'), may hold values from -0.125 to 0.125
- w_down: bfloat16 [128, 384, 2048], P('exp'), may hold values from -0.3125 to 0.3125
Outputs:
- grad_tokens: bfloat16 [32768, 2048], P(('rep', 'exp'))
- grad_prob: bfloat16 [32768, 4], P(('rep', 'exp'))
- grad_gate: bfloat16 [128, 2048, 384], P('exp', 'rep')
- grad_up: bfloat16 [128, 2048, 384], P('exp', 'rep')
- grad_down: bfloat16 [128, 384, 2048], P('exp', 'rep')
Inputs may be any that keep to these rules, and one draw needn't show every extreme that they name: `route`: each row names 4 different experts. In each aligned block of 128 rows (the rows of one device) an expert is named by at most 8 rows; one expert, the same for all blocks, is named by exactly 8 rows of every block.
All inputs are finite; a program needn't handle non-finite values.
Results may differ from a plain program's by a relative error of at most 0.0059.
Values may be sent and summed in bfloat16 or wider, within the bound.
No kernel may reach another device: no remote copies, remote signals or barrier semaphores. Data moves between devices by JAX's collectives and lax.ppermute only.
A program may use at most 128 MiB of HBM per device.

v0:
```python
import functools

import jax
import jax.numpy as jnp
from jax import lax
from jax.experimental import pallas as pl
from jax.experimental.pallas import tpu as pltpu
from jax.sharding import Mesh, PartitionSpec as P


YH, Z, X, C = 2, 8, 4, 2
PLANE = ("yh", "x", "c")
ALL = ("rep", "yh", "z", "x", "c")
PEERS = YH * X * C
CAP = 8
SLOTS = PEERS * CAP
LANES = 128
META = 8
FAR = Z // 2
ROUNDS = (("a0", "a1"), ("b1", "a2", "b2"), ("a3", "b3", "a4"))
BF, F32 = jnp.bfloat16, jnp.float32
SMEM = pl.BlockSpec(memory_space=pltpu.SMEM)
VMEM = pl.BlockSpec(memory_space=pltpu.VMEM)


def params(mib=63):
    return pltpu.CompilerParams(vmem_limit_bytes=mib * 1024 * 1024)


def z_shift(value, step, cross=False):
    pairs = []
    for i in range(Z):
        for core, move in enumerate((step, -step)):
            pairs.append((i * C + core, (i + move) % Z * C + (core ^ cross)))
    return lax.ppermute(value, ("z", "c"), pairs)


def swap(value, axis):
    return lax.ppermute(value, axis, [(0, 1), (1, 0)])


def pack_kernel(route_ref, prob_ref, tokens_ref, grad_ref, out_ref):
    rows, width = tokens_ref.shape
    topk = route_ref.shape[0]
    experts = YH * Z * X * C
    label = lax.broadcasted_iota(jnp.int32, (experts, rows), 0)
    hits = [label == route_ref[k : k + 1, :] for k in range(topk)]
    named = functools.reduce(jnp.logical_or, hits).astype(F32).astype(BF)
    before = lax.broadcasted_iota(jnp.int32, (rows, rows), 0) < lax.broadcasted_iota(
        jnp.int32, (rows, rows), 1
    )
    earlier = jnp.dot(named, before.astype(F32).astype(BF), preferred_element_type=F32)
    out_ref[0:rows, :] = tokens_ref[...]
    out_ref[rows : 2 * rows, :] = grad_ref[...]
    expert = route_ref[...]
    position = jnp.concatenate(
        [jnp.sum(jnp.where(h, earlier, 0.0), axis=0, keepdims=True) for h in hits], axis=0
    )
    per_half = Z * X * C
    slot = (expert // per_half) * (X * C * CAP) + (expert % (X * C)) * CAP
    slot = slot.astype(F32) + position
    plane = ((expert // (X * C)) % Z).astype(F32)
    meta = jnp.concatenate([slot, plane, prob_ref[...].astype(F32)], axis=1)
    meta = jnp.concatenate([meta, jnp.zeros((META - topk, 3 * rows), F32)], axis=0)
    meta = jnp.concatenate([meta, jnp.zeros((META, width - 3 * rows), F32)], axis=1)
    out_ref[2 * rows : 2 * rows + META, :] = meta.astype(BF)


def pack(route, prob, tokens, grad):
    rows, width = tokens.shape
    return pl.pallas_call(
        pack_kernel,
        out_shape=jax.ShapeDtypeStruct((2 * rows + META, width), BF),
        compiler_params=params(),
        name="pack",
    )(route.T, prob.T, tokens, grad)


def slot_hits(meta, z_me, topk):
    rows = LANES
    label = lax.broadcasted_iota(jnp.int32, (SLOTS, rows), 0).astype(F32)
    hits = []
    for k in range(topk):
        slot, plane = meta[k : k + 1, 0:rows], meta[k : k + 1, rows : 2 * rows]
        hits.append((label == slot) & (plane == z_me))
    return hits


def select_rows(meta, z_me, topk):
    hits = slot_hits(meta, z_me, topk)
    return hits, functools.reduce(jnp.logical_or, hits).astype(F32).astype(BF)


def build_kernel(topk, count, z_ref, *refs):
    out_ref = refs[-1]
    z_me = z_ref[0].astype(F32)
    for b in range(count):
        block = refs[b]
        width = block.shape[1]
        meta = block[2 * LANES : 2 * LANES + META, 0 : 3 * LANES].astype(F32)
        hits, select = select_rows(meta, z_me, topk)
        weight = sum(
            jnp.where(h, meta[k : k + 1, 2 * LANES : 3 * LANES], 0.0)
            for k, h in enumerate(hits)
        )
        weight = jnp.sum(weight, axis=1, keepdims=True)
        for part in range(2):
            rows = jnp.dot(
                select, block[part * LANES : (part + 1) * LANES, :], preferred_element_type=F32
            )
            out_ref[:, b, :, part * width : (part + 1) * width] = rows.reshape(
                PEERS, CAP, width
            ).astype(BF)
        out_ref[:, b, :, 2 * width :] = (
            jnp.broadcast_to(weight, (SLOTS, LANES)).reshape(PEERS, CAP, LANES).astype(BF)
        )


def build(z_me, blocks, topk):
    width = blocks[0].shape[1]
    count = len(blocks)
    return pl.pallas_call(
        functools.partial(build_kernel, topk, count),
        in_specs=[SMEM] + [VMEM] * count,
        out_shape=jax.ShapeDtypeStruct((PEERS, count, CAP, 2 * width + LANES), BF),
        compiler_params=params(),
        name="build",
    )(z_me, *blocks)


def expert_kernel(carried, rows_ref, wg_ref, wu_ref, wd_ref, *refs):
    back_ref, x_ref, sc_ref, dg_ref, du_ref = refs[carried:]
    width = wg_ref.shape[0]
    rows = rows_ref[...]
    x_ref[...] = rows[:, 0 : 2 * width]
    x, g = rows[:, 0:width], rows[:, width : 2 * width]
    weight = rows[:, 2 * width : 2 * width + 1].astype(F32)
    last = (((1,), (1,)), ((), ()))
    gate = jnp.dot(x, wg_ref[...], preferred_element_type=F32)
    up = jnp.dot(x, wu_ref[...], preferred_element_type=F32)
    back = lax.dot_general(g, wd_ref[...], last, preferred_element_type=F32)
    sigma = jax.nn.sigmoid(gate)
    active = gate * sigma
    hidden = active * up
    weight_grad = jnp.sum(back * hidden, axis=1, keepdims=True)
    sc_ref[...] = (weight * hidden).astype(BF)
    d_back = weight * back
    d_gate = (d_back * up * sigma * (1.0 + gate * (1.0 - sigma))).astype(BF)
    d_up = (d_back * active).astype(BF)
    dg_ref[...] = d_gate
    du_ref[...] = d_up
    contrib = lax.dot_general(d_gate, wg_ref[...], last, preferred_element_type=F32)
    contrib += lax.dot_general(d_up, wu_ref[...], last, preferred_element_type=F32)
    peers, count, cap, _ = back_ref.shape
    back_ref[:, :, :, 0:width] = contrib.reshape(peers, count, cap, width).astype(BF)
    weight_grad = jnp.broadcast_to(weight_grad, (rows.shape[0], LANES))
    back_ref[:, :, :, width:] = weight_grad.reshape(peers, count, cap, LANES).astype(BF)


def expert(rows, wg, wu, wd, kept, start, total):
    width, hidden = wg.shape
    count = rows.shape[0]
    full = lambda a: pl.BlockSpec(a.shape, lambda i: (0, 0))
    rows_at = lambda n: pl.BlockSpec((count, n), lambda i: (start // count, 0))
    kept_widths = (2 * width, hidden, hidden, hidden)
    back_shape = (PEERS, count // SLOTS, CAP, width + LANES)
    return pl.pallas_call(
        functools.partial(expert_kernel, len(kept)),
        grid=(1,),
        in_specs=[full(rows), full(wg), full(wu), full(wd)]
        + [pl.BlockSpec(memory_space=pl.ANY)] * len(kept),
        out_specs=[pl.BlockSpec(back_shape, lambda i: (0, 0, 0, 0))]
        + [rows_at(n) for n in kept_widths],
        out_shape=[jax.ShapeDtypeStruct(back_shape, BF)]
        + [jax.ShapeDtypeStruct((total, n), BF) for n in kept_widths],
        input_output_aliases={4 + i: 1 + i for i in range(len(kept))},
        compiler_params=params(),
        name="expert",
    )(rows, wg, wu, wd, *kept)


def weights_kernel(rep_ref, x_ref, g_ref, sc_ref, dg_ref, du_ref, *refs):
    keep_g, send_g, keep_u, send_u, keep_d, send_d, down_acc = refs
    step, half_steps = pl.program_id(0), pl.num_programs(0) // 2
    first = (((0,), (0,)), ((), ()))
    x = x_ref[...]
    gate = lax.dot_general(x, dg_ref[...], first, preferred_element_type=F32).astype(BF)
    up = lax.dot_general(x, du_ref[...], first, preferred_element_type=F32).astype(BF)

    @pl.when(step < half_steps)
    def _():
        send_g[...] = gate
        send_u[...] = up

    @pl.when(step >= half_steps)
    def _():
        keep_g[...] = gate
        keep_u[...] = up

    down_acc[...] = lax.dot_general(
        sc_ref[...], g_ref[...], first, preferred_element_type=F32
    )
    half = keep_d.shape[0]
    rep = rep_ref[0]
    keep_d[...] = down_acc[pl.ds(pl.multiple_of(rep * half, half), half), :].astype(BF)
    send_d[...] = down_acc[pl.ds(pl.multiple_of((1 - rep) * half, half), half), :].astype(BF)


def weights(rep, rows, sc, dg, du):
    total, hidden = sc.shape
    width = rows.shape[1] // 2
    tile = 512
    steps = width // tile
    half = steps // 2

    def chosen(i, rep):
        return lax.rem(i + (1 - rep[0]) * half, steps)

    whole = pl.BlockSpec((total, hidden), lambda i, rep: (0, 0), pipeline_mode=pl.Buffered(1))
    keep = pl.BlockSpec((tile, hidden), lambda i, rep: (jnp.maximum(i - half, 0), 0))
    send = pl.BlockSpec((tile, hidden), lambda i, rep: (jnp.minimum(i, half - 1), 0))
    down = pl.BlockSpec((hidden // 2, tile), lambda i, rep: (0, i))
    gu_shape = jax.ShapeDtypeStruct((width // 2, hidden), BF)
    down_shape = jax.ShapeDtypeStruct((hidden // 2, width), BF)
    return pl.pallas_call(
        weights_kernel,
        grid_spec=pltpu.PrefetchScalarGridSpec(
            num_scalar_prefetch=1,
            grid=(steps,),
            in_specs=[
                pl.BlockSpec((total, tile), lambda i, rep: (0, chosen(i, rep))),
                pl.BlockSpec((total, tile), lambda i, rep: (0, steps + i)),
                whole,
                whole,
                whole,
            ],
            out_specs=[keep, send, keep, send, down, down],
            scratch_shapes=[pltpu.VMEM((hidden, tile), F32)],
        ),
        out_shape=[gu_shape] * 4 + [down_shape] * 2,
        compiler_params=params(),
        name="weights",
    )(rep, rows, rows, sc, dg, du)


def combine_kernel(topk, count, z_ref, back_ref, *refs):
    z_me = z_ref[0].astype(F32)
    for b in range(count):
        meta = refs[b][:, 0 : 3 * LANES].astype(F32)
        out_ref = refs[count + b]
        width = out_ref.shape[1]
        hits, select = select_rows(meta, z_me, topk)
        rows = back_ref[:, b, :, 0:width].astype(F32).reshape(SLOTS, width).astype(BF)
        part = lax.dot_general(
            select, rows, (((0,), (0,)), ((), ())), preferred_element_type=F32
        )
        out_ref[0:LANES, :] = part.astype(out_ref.dtype)
        value = back_ref[:, b, :, width:].astype(F32).reshape(SLOTS, LANES)
        grads = [jnp.sum(jnp.where(h, value, 0.0), axis=0, keepdims=True) for h in hits]
        grads.append(jnp.zeros((META - topk, LANES), F32))
        grads = jnp.concatenate(grads, axis=0)
        grads = jnp.concatenate([grads, jnp.zeros((META, width - LANES), F32)], axis=1)
        out_ref[LANES : LANES + META, :] = grads.astype(out_ref.dtype)


def combine(z_me, back, blocks, topk, kinds):
    width = back.shape[-1] - LANES
    count = len(blocks)
    last = blocks[0].shape[0] // META - 1
    return pl.pallas_call(
        functools.partial(combine_kernel, topk, count),
        grid=(1,),
        in_specs=[SMEM, pl.BlockSpec(back.shape, lambda i: (0, 0, 0, 0))]
        + [pl.BlockSpec((META, width), lambda i: (last, 0))] * count,
        out_specs=[pl.BlockSpec((LANES + META, width), lambda i: (0, 0))] * count,
        out_shape=[jax.ShapeDtypeStruct((LANES + META, width), k) for k in kinds],
        compiler_params=params(),
        name="combine",
    )(z_me, back, *blocks)


def plane_exchange(value):
    return lax.all_to_all(value, PLANE, split_axis=0, concat_axis=0, tiled=True)


def body(tokens, out_grad, route, prob, w_gate, w_up, w_down):
    local, _ = tokens.shape
    topk = route.shape[1]
    wg, wu, wd = w_gate[0], w_up[0], w_down[0]
    z_me = lax.axis_index("z").reshape(1)
    rep = lax.axis_index("rep").reshape(1)

    blocks = {"a0": pack(route, prob, tokens, out_grad)}
    blocks["a1"] = z_shift(blocks["a0"], 1)
    blocks["b0"] = swap(blocks["a0"], "c")
    for s in range(1, FAR + 1):
        for kind in "ab":
            name = f"{kind}{s}"
            if name not in blocks and name != f"b{FAR}":
                blocks[name] = z_shift(blocks[f"{kind}{s - 1}"], 1)

    kept, backs = [], []
    starts = (6 * SLOTS, 3 * SLOTS, 0)
    for i, group in enumerate(ROUNDS):
        sent = build(z_me, [blocks[r] for r in group], topk)
        rows = plane_exchange(sent)
        rows = rows.reshape(-1, rows.shape[-1])
        back, *kept = expert(rows, wg, wu, wd, kept, starts[i], Z * SLOTS)
        backs.append(back)
    halves = weights(rep, *kept)
    grads = []
    for name, keep, send in zip(("gate", "up", "down"), halves[0::2], halves[1::2]):
        got = swap(send, "rep")
        grads.append((keep.astype(F32) + got.astype(F32)).astype(BF)[None])

    partial = {}
    for i in range(len(ROUNDS) - 1, -1, -1):
        returned = plane_exchange(backs[i])
        group = ROUNDS[i]
        kinds = [F32 if r == "a0" else BF for r in group]
        parts = combine(z_me, returned, [blocks[r] for r in group], topk, kinds)
        partial.update(zip(group, parts))
    moving = {"a": partial[f"a{FAR}"], "b": partial[f"b{FAR - 1}"]}
    for s in range(FAR - 1, -1, -1):
        for kind in "ab":
            if f"{kind}{s}" == f"b{FAR - 1}":
                continue
            came = z_shift(moving[kind], -1, cross=kind + str(s) == "b0")
            if s > 0:
                came = (partial[f"{kind}{s}"].astype(F32) + came.astype(F32)).astype(BF)
            moving[kind] = came
    ends = (partial["a0"], moving["a"], moving["b"])
    grad_tokens = sum(e[:local].astype(F32) for e in ends).astype(BF)
    grad_prob = sum(e[local : local + topk, :local].astype(F32) for e in ends).T.astype(BF)
    return (grad_tokens, grad_prob, *grads)


def solution(mesh):
    fine = Mesh(mesh.devices.reshape(-1, YH, Z, X, C), ALL)
    exp = ("yh", "z", "x", "c")
    placed = (P(ALL, None),) * 4 + (P(exp, None, None),) * 3
    return jax.shard_map(
        body,
        mesh=fine,
        in_specs=placed,
        out_specs=(P(ALL, None),) * 2 + (P(exp, "rep", None),) * 3,
        check_vma=False,
    )
```

profile of v0, /device:TPU:1, one launch (start us, length us, event | category | flops | bytes accessed | tf_op | source)
XLA Modules:
  0.0 314.3 jit_solution(14558746954633943722)
XLA Ops:
  0.6 2.5 pack.1.refs_0_
  3.1 3.2 %collective-permute-start.1 = (bf16[264,2048]{1,0:T(8,128)(2,1)}, bf16[264,2048]{1,0:T(8,128)(2,1)}, u32[]{:S(2)}, u32[]{:S(2)}) collective-permute-start(bf16[264,2048]{1,0:T(8,128)(2,1)} %pack.1.refs_0_), channel_id=1, source_target_pairs={{0,1},{1,0},{2,3},{3,2},{4,5},{5,4},{6,7},{7,6},{8,9},{9,8},{10,11... | collective-permute-start | bytes 3244040 | tf_op jit(solution)/shard_map/ppermute | solution.py:39
  6.3 3.9 %collective-permute-start = (bf16[264,2048]{1,0:T(8,128)(2,1)}, bf16[264,2048]{1,0:T(8,128)(2,1)}, u32[]{:S(2)}, u32[]{:S(2)}) collective-permute-start(bf16[264,2048]{1,0:T(8,128)(2,1)} %pack.1.refs_0_), channel_id=1, source_target_pairs={{0,8},{1,57},{8,16},{9,1},{16,24},{17,9},{24,32},{25,17},{32,40},{... | collective-permute-start | bytes 3244040 | tf_op jit(solution)/shard_map/ppermute | solution.py:35
  10.2 2.7 collective-permute-start.2
  12.9 9.7 %collective-permute-done.refs_1_ = bf16[264,2048]{1,0:T(8,128)(2,1)} collective-permute-done((bf16[264,2048]{1,0:T(8,128)(2,1)}, bf16[264,2048]{1,0:T(8,128)(2,1)}, u32[]{:S(2)}, u32[]{:S(2)}) %collective-permute-start) | collective-permute-done | bytes 1081376 | tf_op jit(solution)/shard_map/ppermute | solution.py:35
  22.6 3.7 %build.3 = bf16[16,2,8,4224]{3,2,1,0:T(8,128)(2,1)} custom-call(s32[1]{0:T(128)} %bitcast.z_ref, bf16[264,2048]{1,0:T(8,128)(2,1)} %pack.1.refs_0_, bf16[264,2048]{1,0:T(8,128)(2,1)} %collective-permute-done.refs_1_), custom_call_target="tpu_custom_call" | custom-call | tf_op jit(solution)/shard_map/build/pallas_call | solution.py:122
  26.3 8.3 %all-to-all-start = ((bf16[16,2,8,4224]{3,2,1,0:T(8,128)(2,1)}), bf16[16,2,8,4224]{3,2,1,0:T(8,128)(2,1)}, u32[]{:S(2)}, u32[]{:S(2)}) async-start(bf16[16,2,8,4224]{3,2,1,0:T(8,128)(2,1)} %build.3), calls=%async_computation | async-start | bytes 4325376 | tf_op jit(solution)/shard_map/all_to_all | solution.py:283
  34.5 1.9 collective-permute-start.3
  36.4 0.8 collective-permute-start.4
  37.3 11.8 %collective-permute-done.3.refs_1_ = bf16[264,2048]{1,0:T(8,128)(2,1)} collective-permute-done((bf16[264,2048]{1,0:T(8,128)(2,1)}, bf16[264,2048]{1,0:T(8,128)(2,1)}, u32[]{:S(2)}, u32[]{:S(2)}) %collective-permute-start.3) | collective-permute-done | bytes 1081376 | tf_op jit(solution)/shard_map/ppermute | solution.py:35
  49.1 11.6 %collective-permute-done.4.refs_2_ = bf16[264,2048]{1,0:T(8,128)(2,1)} collective-permute-done((bf16[264,2048]{1,0:T(8,128)(2,1)}, bf16[264,2048]{1,0:T(8,128)(2,1)}, u32[]{:S(2)}, u32[]{:S(2)}) %collective-permute-start.4) | collective-permute-done | bytes 1081376 | tf_op jit(solution)/shard_map/ppermute | solution.py:35
  60.7 4.6 %build.4 = bf16[16,3,8,4224]{3,2,1,0:T(8,128)(2,1)} custom-call(s32[1]{0:T(128)} %bitcast.z_ref, bf16[264,2048]{1,0:T(8,128)(2,1)} %collective-permute-done.2.refs_0_, bf16[264,2048]{1,0:T(8,128)(2,1)} %collective-permute-done.3.refs_1_, bf16[264,2048]{1,0:T(8,128)(2,1)} %collective-permute-done.4.refs_2_), custom_call_target="tpu_custom_call" | custom-call | tf_op jit(solution)/shard_map/build/pallas_call | solution.py:122
  65.3 9.3 %all-to-all-start.2 = ((bf16[16,3,8,4224]{3,2,1,0:T(8,128)(2,1)}), bf16[16,3,8,4224]{3,2,1,0:T(8,128)(2,1)}, u32[]{:S(2)}, u32[]{:S(2)}) async-start(bf16[16,3,8,4224]{3,2,1,0:T(8,128)(2,1)} %build.4), calls=%async_computation.2 | async-start | bytes 6488064 | tf_op jit(solution)/shard_map/all_to_all | solution.py:283
  74.6 0.7 collective-permute-start.5
  75.9 13.3 %collective-permute-done.5.refs_0_ = bf16[264,2048]{1,0:T(8,128)(2,1)S(1)} collective-permute-done((bf16[264,2048]{1,0:T(8,128)(2,1)}, bf16[264,2048]{1,0:T(8,128)(2,1)S(1)}, u32[]{:S(2)}, u32[]{:S(2)}) %collective-permute-start.5) | collective-permute-done | bytes 1081376 | tf_op jit(solution)/shard_map/ppermute | solution.py:35
  89.3 1.0 copy-done
  90.2 1.9 collective-permute-start.7
  92.2 8.7 %collective-permute-done.6.refs_1_ = bf16[264,2048]{1,0:T(8,128)(2,1)} collective-permute-done((bf16[264,2048]{1,0:T(8,128)(2,1)}, bf16[264,2048]{1,0:T(8,128)(2,1)}, u32[]{:S(2)}, u32[]{:S(2)}) %collective-permute-start.6) | collective-permute-done | bytes 1081376 | tf_op jit(solution)/shard_map/ppermute | solution.py:35
  100.8 11.6 %collective-permute-done.7.refs_2_ = bf16[264,2048]{1,0:T(8,128)(2,1)} collective-permute-done((bf16[264,2048]{1,0:T(8,128)(2,1)S(1)}, bf16[264,2048]{1,0:T(8,128)(2,1)}, u32[]{:S(2)}, u32[]{:S(2)}) %collective-permute-start.7) | collective-permute-done | bytes 1081376 | tf_op jit(solution)/shard_map/ppermute | solution.py:35
  112.4 4.6 %build.5 = bf16[16,3,8,4224]{3,2,1,0:T(8,128)(2,1)} custom-call(s32[1]{0:T(128)} %bitcast.z_ref, bf16[264,2048]{1,0:T(8,128)(2,1)} %copy-done, bf16[264,2048]{1,0:T(8,128)(2,1)} %collective-permute-done.6.refs_1_, bf16[264,2048]{1,0:T(8,128)(2,1)} %collective-permute-done.7.refs_2_), custom_call_target="tpu_custom_call" | custom-call | tf_op jit(solution)/shard_map/build/pallas_call | solution.py:122
  117.1 0.8 all-to-all-done.2
  117.9 8.5 %all-to-all-start.4 = ((bf16[16,3,8,4224]{3,2,1,0:T(8,128)(2,1)}), bf16[16,3,8,4224]{3,2,1,0:T(8,128)(2,1)}, u32[]{:S(2)}, u32[]{:S(2)}) async-start(bf16[16,3,8,4224]{3,2,1,0:T(8,128)(2,1)} %build.5), calls=%async_computation.4 | async-start | bytes 6488064 | tf_op jit(solution)/shard_map/all_to_all | solution.py:283
  126.4 7.1 %expert.3 = (bf16[16,2,8,2176]{3,2,1,0:T(8,128)(2,1)}, bf16[1024,4096]{1,0:T(8,128)(2,1)}, bf16[1024,384]{1,0:T(8,128)(2,1)}, bf16[1024,384]{1,0:T(8,128)(2,1)}, bf16[1024,384]{1,0:T(8,128)(2,1)}) custom-call(bf16[256,4224]{1,0:T(8,128)(2,1)} %bitcast.3.rows_ref, bf16[2048,384]{1,0:T(8,128)(2,1)} %bitcast.18, bf16[2048,384]{1,0:T(8,128)(2,1)} %bitcast.21, ...), custom_call_target="tpu_custom_call" | custom-call | tf_op jit(solution)/shard_map/expert/pallas_call | solution.py:167
  133.4 36.1 %all-to-all-done.4 = bf16[16,3,8,4224]{3,2,1,0:T(8,128)(2,1)} async-done(((bf16[16,3,8,4224]{3,2,1,0:T(8,128)(2,1)}), bf16[16,3,8,4224]{3,2,1,0:T(8,128)(2,1)}, u32[]{:S(2)}, u32[]{:S(2)}) %all-to-all-start.4) | async-done | bytes 3244064 | tf_op jit(solution)/shard_map/all_to_all | solution.py:283
  169.6 6.1 %all-to-all-start.1 = ((bf16[16,2,8,2176]{3,2,1,0:T(8,128)(2,1)}), bf16[16,2,8,2176]{3,2,1,0:T(8,128)(2,1)}, u32[]{:S(2)}, u32[]{:S(2)}) async-start(bf16[16,2,8,2176]{3,2,1,0:T(8,128)(2,1)} %get-tuple-element.34), calls=%async_computation.1 | async-start | bytes 2228224 | tf_op jit(solution)/shard_map/all_to_all | solution.py:283
  175.7 9.0 %expert.4 = (bf16[16,3,8,2176]{3,2,1,0:T(8,128)(2,1)}, bf16[1024,4096]{1,0:T(8,128)(2,1)}, bf16[1024,384]{1,0:T(8,128)(2,1)}, bf16[1024,384]{1,0:T(8,128)(2,1)}, bf16[1024,384]{1,0:T(8,128)(2,1)}) custom-call(bf16[384,4224]{1,0:T(8,128)(2,1)} %bitcast.7.rows_ref, ...), custom_call_target="tpu_custom_call", output_to_operand_aliasing={{1}: (4, {}), {2}: (5, {}), {3}: (6, {}), {4}: (7, {})} | custom-call | tf_op jit(solution)/shard_map/expert/pallas_call | solution.py:167
  184.7 9.0 %expert.5 = (bf16[16,3,8,2176]{3,2,1,0:T(8,128)(2,1)}, bf16[1024,4096]{1,0:T(8,128)(2,1)}, bf16[1024,384]{1,0:T(8,128)(2,1)}, bf16[1024,384]{1,0:T(8,128)(2,1)}, bf16[1024,384]{1,0:T(8,128)(2,1)}) custom-call(bf16[384,4224]{1,0:T(8,128)(2,1)} %bitcast.8.rows_ref, ...), custom_call_target="tpu_custom_call", output_to_operand_aliasing={{1}: (4, {}), {2}: (5, {}), {3}: (6, {}), {4}: (7, {})} | custom-call | tf_op jit(solution)/shard_map/expert/pallas_call | solution.py:167
  193.8 31.4 %all_to_all.30.back_ref = bf16[16,3,8,2176]{3,2,1,0:T(8,128)(2,1)} all-to-all(bf16[16,3,8,2176]{3,2,1,0:T(8,128)(2,1)} %get-tuple-element.47), channel_id=1, replica_groups=mesh['rep'=2,'yh'=2,'z'=8,'x'=4,'c'=2] {'yh','x','c'}, dimensions={0} | all-to-all | bytes 3342336 | tf_op jit(solution)/shard_map/all_to_all | solution.py:283
  225.2 4.5 %all-to-all-start.3 = ((bf16[16,3,8,2176]{3,2,1,0:T(8,128)(2,1)}), bf16[16,3,8,2176]{3,2,1,0:T(8,128)(2,1)}, u32[]{:S(2)}, u32[]{:S(2)}) async-start(bf16[16,3,8,2176]{3,2,1,0:T(8,128)(2,1)} %get-tuple-element.41), calls=%async_computation.3 | async-start | bytes 3342336 | tf_op jit(solution)/shard_map/all_to_all | solution.py:283
  229.7 3.1 combine.5
  232.8 10.2 %collective-permute-done.8 = bf16[136,2048]{1,0:T(8,128)(2,1)S(1)} collective-permute-done((bf16[136,2048]{1,0:T(8,128)(2,1)}, bf16[136,2048]{1,0:T(8,128)(2,1)S(1)}, u32[]{:S(2)}, u32[]{:S(2)}) %collective-permute-start.8) | collective-permute-done | bytes 557088 | tf_op jit(solution)/shard_map/ppermute | solution.py:35
  243.0 2.0 add_convert_fusion.7
  245.0 2.9 combine.3
  247.9 11.5 %weights.1 = (bf16[1024,384]{1,0:T(8,128)(2,1)}, bf16[1024,384]{1,0:T(8,128)(2,1)}, bf16[1024,384]{1,0:T(8,128)(2,1)}, bf16[1024,384]{1,0:T(8,128)(2,1)}, bf16[1...) custom-call(s32[1]{0:T(128)} %bitcast.10.rep_ref, bf16[1024,4096]{1,0:T(8,128)(2,1)} %get-tuple-element.53.x_ref.g_ref, ...), custom_call_target="tpu_custom_call" | custom-call | tf_op jit(solution)/shard_map/weights/pallas_call | solution.py:225
  259.8 1.1 collective-permute-start.16
  261.3 3.0 combine.4
  264.3 1.4 add_convert_fusion.4
  265.8 1.3 add_convert_fusion.6
  267.1 1.7 collective-permute-start.10
  268.8 9.0 %collective-permute-done.15 = bf16[1024,384]{1,0:T(8,128)(2,1)} collective-permute-done((bf16[1024,384]{1,0:T(8,128)(2,1)}, bf16[1024,384]{1,0:T(8,128)(2,1)}, u32[]{:S(2)}, u32[]{:S(2)}) %collective-permute-start.15) | collective-permute-done | bytes 786464 | tf_op jit(solution)/shard_map/ppermute | solution.py:39
  277.8 2.3 fusion
  280.2 3.9 %collective-permute-start.14 = (bf16[136,2048]{1,0:T(8,128)(2,1)S(1)}, bf16[136,2048]{1,0:T(8,128)(2,1)S(1)}, u32[]{:S(2)}, u32[]{:S(2)}) collective-permute-start(bf16[136,2048]{1,0:T(8,128)(2,1)S(1)} %add_convert_fusion.3), channel_id=1, source_target_pairs={{0,57},{1,8},{8,1},{9,16},{16,9},{17,24},{24,17},{25,32},{32,25},{... | collective-permute-start | bytes 1671176 | tf_op jit(solution)/shard_map/ppermute | solution.py:35
  284.3 10.3 %collective-permute-done.16 = bf16[1024,384]{1,0:T(8,128)(2,1)} collective-permute-done((bf16[1024,384]{1,0:T(8,128)(2,1)}, bf16[1024,384]{1,0:T(8,128)(2,1)}, u32[]{:S(2)}, u32[]{:S(2)}) %collective-permute-start.16) | collective-permute-done | bytes 786464 | tf_op jit(solution)/shard_map/ppermute | solution.py:39
  294.6 2.3 fusion.1
  296.9 14.5 %collective-permute-done.17 = bf16[192,2048]{1,0:T(8,128)(2,1)S(1)} collective-permute-done((bf16[192,2048]{1,0:T(8,128)(2,1)}, bf16[192,2048]{1,0:T(8,128)(2,1)S(1)}, u32[]{:S(2)}, u32[]{:S(2)}) %collective-permute-start.17) | collective-permute-done | bytes 786464 | tf_op jit(solution)/shard_map/ppermute | solution.py:39
  311.4 1.2 fusion.2
  312.8 0.6 fusion.3
  313.3 1.0 add_convert_fusion.8
  (36 shorter events, 2.1 us)
Async XLA Ops:
  3.1 7.1 %collective-permute-start.1 = (bf16[264,2048]{1,0:T(8,128)(2,1)}, bf16[264,2048]{1,0:T(8,128)(2,1)}, u32[]{:S(2)}, u32[]{:S(2)}) collective-permute-start(bf16[264,2048]{1,0:T(8,128)(2,1)} %pack.1.refs_0_), channel_id=1, source_target_pairs={{0,1},{1,0},{2,3},{3,2},{4,5},{5,4},{6,7},{7,6},{8,9},{9,8},{10,11... | collective-permute-start | bytes 3244040 | tf_op jit(solution)/shard_map/ppermute | solution.py:39
  6.3 16.3 %collective-permute-start = (bf16[264,2048]{1,0:T(8,128)(2,1)}, bf16[264,2048]{1,0:T(8,128)(2,1)}, u32[]{:S(2)}, u32[]{:S(2)}) collective-permute-start(bf16[264,2048]{1,0:T(8,128)(2,1)} %pack.1.refs_0_), channel_id=1, source_target_pairs={{0,8},{1,57},{8,16},{9,1},{16,24},{17,9},{24,32},{25,17},{32,40},{... | collective-permute-start | bytes 3244040 | tf_op jit(solution)/shard_map/ppermute | solution.py:35
  10.2 26.3 %collective-permute-start.2 = (bf16[264,2048]{1,0:T(8,128)(2,1)}, bf16[264,2048]{1,0:T(8,128)(2,1)}, u32[]{:S(2)}, u32[]{:S(2)}) collective-permute-start(bf16[264,2048]{1,0:T(8,128)(2,1)} %collective-permute-done.1), channel_id=1, source_target_pairs={{0,8},{1,57},{8,16},{9,1},{16,24},{17,9},{24,32},{25,17},{32,40},{... | collective-permute-start | bytes 3244040 | tf_op jit(solution)/shard_map/ppermute | solution.py:35
  26.3 39.1 %all-to-all-start = ((bf16[16,2,8,4224]{3,2,1,0:T(8,128)(2,1)}), bf16[16,2,8,4224]{3,2,1,0:T(8,128)(2,1)}, u32[]{:S(2)}, u32[]{:S(2)}) async-start(bf16[16,2,8,4224]{3,2,1,0:T(8,128)(2,1)} %build.3), calls=%async_computation | async-start | bytes 4325376 | tf_op jit(solution)/shard_map/all_to_all | solution.py:283
  34.5 14.6 %collective-permute-start.3 = (bf16[264,2048]{1,0:T(8,128)(2,1)}, bf16[264,2048]{1,0:T(8,128)(2,1)}, u32[]{:S(2)}, u32[]{:S(2)}) collective-permute-start(bf16[264,2048]{1,0:T(8,128)(2,1)} %collective-permute-done.refs_1_), channel_id=1, source_target_pairs={{0,8},{1,57},{8,16},{9,1},{16,24},{17,9},{24,32},{25,17},{32,40},{... | collective-permute-start | bytes 3244040 | tf_op jit(solution)/shard_map/ppermute | solution.py:35
  36.4 24.3 %collective-permute-start.4 = (bf16[264,2048]{1,0:T(8,128)(2,1)}, bf16[264,2048]{1,0:T(8,128)(2,1)}, u32[]{:S(2)}, u32[]{:S(2)}) collective-permute-start(bf16[264,2048]{1,0:T(8,128)(2,1)} %collective-permute-done.2.refs_0_), channel_id=1, source_target_pairs={{0,8},{1,57},{8,16},{9,1},{16,24},{17,9},{24,32},{25,17},{32,40},{... | collective-permute-start | bytes 3244040 | tf_op jit(solution)/shard_map/ppermute | solution.py:35
  65.3 52.5 %all-to-all-start.2 = ((bf16[16,3,8,4224]{3,2,1,0:T(8,128)(2,1)}), bf16[16,3,8,4224]{3,2,1,0:T(8,128)(2,1)}, u32[]{:S(2)}, u32[]{:S(2)}) async-start(bf16[16,3,8,4224]{3,2,1,0:T(8,128)(2,1)} %build.4), calls=%async_computation.2 | async-start | bytes 6488064 | tf_op jit(solution)/shard_map/all_to_all | solution.py:283
  74.6 14.6 %collective-permute-start.5 = (bf16[264,2048]{1,0:T(8,128)(2,1)}, bf16[264,2048]{1,0:T(8,128)(2,1)S(1)}, u32[]{:S(2)}, u32[]{:S(2)}) collective-permute-start(bf16[264,2048]{1,0:T(8,128)(2,1)} %collective-permute-done.3.refs_1_), channel_id=1, source_target_pairs={{0,8},{1,57},{8,16},{9,1},{16,24},{17,9},{24,32},{25,17},{32,40},{... | collective-permute-start | bytes 3244040 | tf_op jit(solution)/shard_map/ppermute | solution.py:35
  75.3 25.5 %collective-permute-start.6 = (bf16[264,2048]{1,0:T(8,128)(2,1)}, bf16[264,2048]{1,0:T(8,128)(2,1)}, u32[]{:S(2)}, u32[]{:S(2)}) collective-permute-start(bf16[264,2048]{1,0:T(8,128)(2,1)} %collective-permute-done.4.refs_2_), channel_id=1, source_target_pairs={{0,8},{1,57},{8,16},{9,1},{16,24},{17,9},{24,32},{25,17},{32,40},{... | collective-permute-start | bytes 3244040 | tf_op jit(solution)/shard_map/ppermute | solution.py:35
  89.3 1.0 copy-start
  90.2 22.2 %collective-permute-start.7 = (bf16[264,2048]{1,0:T(8,128)(2,1)S(1)}, bf16[264,2048]{1,0:T(8,128)(2,1)}, u32[]{:S(2)}, u32[]{:S(2)}) collective-permute-start(bf16[264,2048]{1,0:T(8,128)(2,1)S(1)} %collective-permute-done.5.refs_0_), channel_id=1, source_target_pairs={{0,8},{1,57},{8,16},{9,1},{16,24},{17,9},{24,32},{25,17},{32,40},{... | collective-permute-start | bytes 3244040 | tf_op jit(solution)/shard_map/ppermute | solution.py:35
  117.9 51.7 %all-to-all-start.4 = ((bf16[16,3,8,4224]{3,2,1,0:T(8,128)(2,1)}), bf16[16,3,8,4224]{3,2,1,0:T(8,128)(2,1)}, u32[]{:S(2)}, u32[]{:S(2)}) async-start(bf16[16,3,8,4224]{3,2,1,0:T(8,128)(2,1)} %build.5), calls=%async_computation.4 | async-start | bytes 6488064 | tf_op jit(solution)/shard_map/all_to_all | solution.py:283
  169.6 24.2 %all-to-all-start.1 = ((bf16[16,2,8,2176]{3,2,1,0:T(8,128)(2,1)}), bf16[16,2,8,2176]{3,2,1,0:T(8,128)(2,1)}, u32[]{:S(2)}, u32[]{:S(2)}) async-start(bf16[16,2,8,2176]{3,2,1,0:T(8,128)(2,1)} %get-tuple-element.34), calls=%async_computation.1 | async-start | bytes 2228224 | tf_op jit(solution)/shard_map/all_to_all | solution.py:283
  225.2 36.1 %all-to-all-start.3 = ((bf16[16,3,8,2176]{3,2,1,0:T(8,128)(2,1)}), bf16[16,3,8,2176]{3,2,1,0:T(8,128)(2,1)}, u32[]{:S(2)}, u32[]{:S(2)}) async-start(bf16[16,3,8,2176]{3,2,1,0:T(8,128)(2,1)} %get-tuple-element.41), calls=%async_computation.3 | async-start | bytes 3342336 | tf_op jit(solution)/shard_map/all_to_all | solution.py:283
  232.8 10.2 %collective-permute-start.8 = (bf16[136,2048]{1,0:T(8,128)(2,1)}, bf16[136,2048]{1,0:T(8,128)(2,1)S(1)}, u32[]{:S(2)}, u32[]{:S(2)}) collective-permute-start(bf16[136,2048]{1,0:T(8,128)(2,1)} %get-tuple-element.49), channel_id=1, source_target_pairs={{0,56},{1,9},{8,0},{9,17},{16,8},{17,25},{24,16},{25,33},{32,24},{... | collective-permute-start | bytes 1671176 | tf_op jit(solution)/shard_map/ppermute | solution.py:35
  232.8 31.5 %collective-permute-start.12 = (bf16[136,2048]{1,0:T(8,128)(2,1)}, bf16[136,2048]{1,0:T(8,128)(2,1)}, u32[]{:S(2)}, u32[]{:S(2)}) collective-permute-start(bf16[136,2048]{1,0:T(8,128)(2,1)} %get-tuple-element.52), channel_id=1, source_target_pairs={{0,56},{1,9},{8,0},{9,17},{16,8},{17,25},{24,16},{25,33},{32,24},{... | collective-permute-start | bytes 1671176 | tf_op jit(solution)/shard_map/ppermute | solution.py:35
  245.0 20.8 %collective-permute-start.9 = (bf16[136,2048]{1,0:T(8,128)(2,1)}, bf16[136,2048]{1,0:T(8,128)(2,1)}, u32[]{:S(2)}, u32[]{:S(2)}) collective-permute-start(bf16[136,2048]{1,0:T(8,128)(2,1)} %add_convert_fusion.7), channel_id=1, source_target_pairs={{0,56},{1,9},{8,0},{9,17},{16,8},{17,25},{24,16},{25,33},{32,24},{... | collective-permute-start | bytes 1671176 | tf_op jit(solution)/shard_map/ppermute | solution.py:35
  259.4 18.4 %collective-permute-start.15 = (bf16[1024,384]{1,0:T(8,128)(2,1)}, bf16[1024,384]{1,0:T(8,128)(2,1)}, u32[]{:S(2)}, u32[]{:S(2)}) collective-permute-start(bf16[1024,384]{1,0:T(8,128)(2,1)} %get-tuple-element.58), channel_id=1, source_target_pairs={{0,128},{128,0},{1,129},{129,1},{2,130},{130,2},{3,131},{131,3},{4... | collective-permute-start | bytes 2359304 | tf_op jit(solution)/shard_map/ppermute | solution.py:39
  259.8 34.9 %collective-permute-start.16 = (bf16[1024,384]{1,0:T(8,128)(2,1)}, bf16[1024,384]{1,0:T(8,128)(2,1)}, u32[]{:S(2)}, u32[]{:S(2)}) collective-permute-start(bf16[1024,384]{1,0:T(8,128)(2,1)} %get-tuple-element.60), channel_id=1, source_target_pairs={{0,128},{128,0},{1,129},{129,1},{2,130},{130,2},{3,131},{131,3},{4... | collective-permute-start | bytes 2359304 | tf_op jit(solution)/shard_map/ppermute | solution.py:39
  260.9 50.5 %collective-permute-start.17 = (bf16[192,2048]{1,0:T(8,128)(2,1)}, bf16[192,2048]{1,0:T(8,128)(2,1)S(1)}, u32[]{:S(2)}, u32[]{:S(2)}) collective-permute-start(bf16[192,2048]{1,0:T(8,128)(2,1)} %get-tuple-element.62), channel_id=1, source_target_pairs={{0,128},{128,0},{1,129},{129,1},{2,130},{130,2},{3,131},{131,3},{4... | collective-permute-start | bytes 2359304 | tf_op jit(solution)/shard_map/ppermute | solution.py:39
  264.3 1.5 copy-start.7
  265.7 12.1 %copy-start.4 = (bf16[1024,384]{1,0:T(8,128)(2,1)S(1)}, bf16[1024,384]{1,0:T(8,128)(2,1)}, u32[]{:S(2)}) copy-start(bf16[1024,384]{1,0:T(8,128)(2,1)} %get-tuple-element.57) | copy-start | bytes 2359300
  265.7 14.4 %collective-permute-start.13 = (bf16[136,2048]{1,0:T(8,128)(2,1)S(1)}, bf16[136,2048]{1,0:T(8,128)(2,1)S(1)}, u32[]{:S(2)}, u32[]{:S(2)}) collective-permute-start(bf16[136,2048]{1,0:T(8,128)(2,1)S(1)} %add_convert_fusion.4), channel_id=1, source_target_pairs={{0,56},{1,9},{8,0},{9,17},{16,8},{17,25},{24,16},{25,33},{32,24},{... | collective-permute-start | bytes 1671176 | tf_op jit(solution)/shard_map/ppermute | solution.py:35
  267.1 17.0 %collective-permute-start.10 = (bf16[136,2048]{1,0:T(8,128)(2,1)S(1)}, bf16[136,2048]{1,0:T(8,128)(2,1)S(1)}, u32[]{:S(2)}, u32[]{:S(2)}) collective-permute-start(bf16[136,2048]{1,0:T(8,128)(2,1)S(1)} %add_convert_fusion.6), channel_id=1, source_target_pairs={{0,56},{1,9},{8,0},{9,17},{16,8},{17,25},{24,16},{25,33},{32,24},{... | collective-permute-start | bytes 1671176 | tf_op jit(solution)/shard_map/ppermute | solution.py:35
  277.8 2.3 copy-start.6
  280.1 4.0 %copy-start.5 = (bf16[136,2048]{1,0:T(8,128)(2,1)S(1)}, bf16[136,2048]{1,0:T(8,128)(2,1)}, u32[]{:S(2)}) copy-start(bf16[136,2048]{1,0:T(8,128)(2,1)} %get-tuple-element.36) | copy-start | bytes 1671172
  280.2 14.4 %copy-start.3 = (bf16[1024,384]{1,0:T(8,128)(2,1)S(1)}, bf16[1024,384]{1,0:T(8,128)(2,1)}, u32[]{:S(2)}) copy-start(bf16[1024,384]{1,0:T(8,128)(2,1)} %get-tuple-element.59) | copy-start | bytes 2359300
  280.2 32.3 %collective-permute-start.14 = (bf16[136,2048]{1,0:T(8,128)(2,1)S(1)}, bf16[136,2048]{1,0:T(8,128)(2,1)S(1)}, u32[]{:S(2)}, u32[]{:S(2)}) collective-permute-start(bf16[136,2048]{1,0:T(8,128)(2,1)S(1)} %add_convert_fusion.3), channel_id=1, source_target_pairs={{0,57},{1,8},{8,1},{9,16},{16,9},{17,24},{24,17},{25,32},{32,25},{... | collective-permute-start | bytes 1671176 | tf_op jit(solution)/shard_map/ppermute | solution.py:35
  284.2 28.3 %collective-permute-start.11 = (bf16[136,2048]{1,0:T(8,128)(2,1)S(1)}, bf16[136,2048]{1,0:T(8,128)(2,1)S(1)}, u32[]{:S(2)}, u32[]{:S(2)}) collective-permute-start(bf16[136,2048]{1,0:T(8,128)(2,1)S(1)} %add_convert_fusion.5), channel_id=1, source_target_pairs={{0,56},{1,9},{8,0},{9,17},{16,8},{17,25},{24,16},{25,33},{32,24},{... | collective-permute-start | bytes 1671176 | tf_op jit(solution)/shard_map/ppermute | solution.py:35
  294.6 16.7 %copy-start.2 = (bf16[192,2048]{1,0:T(8,128)(2,1)S(1)}, bf16[192,2048]{1,0:T(8,128)(2,1)}, u32[]{:S(2)}) copy-start(bf16[192,2048]{1,0:T(8,128)(2,1)} %get-tuple-element.61) | copy-start | bytes 2359300
  311.4 1.4 copy-start.1
where the time goes:
time: 316 us; the launch traced here: 314 us
  waiting for transfers between devices  148 us (47%)
  Pallas kernels  60.9 us (19%)
  starting transfers between devices  60 us (19%)
  blocking collectives  31.4 us (10%)
  other arithmetic  12.2 us (4%)
    ppermute x14, waiting for transfers between devices, z_shift(): return lax.ppermute(value, ('z', 'c'), pairs)  77 us
    all_to_all x5, waiting for transfers between devices, plane_exchange(): return lax.all_to_all(value, PLANE, split_axis=0, concat_axis=0, tiled=True)  37 us
    all_to_all x5, starting transfers between devices, plane_exchange(): return lax.all_to_all(value, PLANE, split_axis=0, concat_axis=0, tiled=True)  36.7 us
    ppermute x4, waiting for transfers between devices, swap(): return lax.ppermute(value, axis, [(0, 1), (1, 0)])  33.8 us
    all_to_all x1, blocking collectives, plane_exchange(): return lax.all_to_all(value, PLANE, split_axis=0, concat_axis=0, tiled=True)  31.4 us
    pallas_call x3, Pallas kernels, expert(): pl.pallas_call(functools.partial(expert_kernel, len(kept)), grid=(1,), in...  25.1 us
    ppermute x14, starting transfers between devices, z_shift(): return lax.ppermute(value, ('z', 'c'), pairs)  18.2 us
    pallas_call x3, Pallas kernels, build(): pl.pallas_call(functools.partial(build_kernel, topk, count), in_specs=[SM...  12.9 us
  transfers between devices with their start and end apart: 23, of which 13 were waited for; matrix products, arithmetic and copies ran while one was open for 3% of the time, Pallas kernels for 19%

commit v1 on v0

--- a/solution.py
+++ b/solution.py
@@ -17,7 +17,12 @@
 LANES = 128
 META = 8
 FAR = Z // 2
-ROUNDS = (("a0", "a1"), ("b1", "a2", "b2"), ("a3", "b3", "a4"))
+ROUNDS = (
+    (("a0", "a1"), 6, ((0, 0, 1), (1, 3, 1))),
+    (("b1", "a2", "b2"), 3, ((1, 0, 3),)),
+    (("a3", "b3", "a4"), 0, ((2, 0, 3),)),
+)
+RETURNS = (("a0",), ("b1", "a2", "b2", "a1"), ("a3", "b3", "a4"))
 BF, F32 = jnp.bfloat16, jnp.float32
 SMEM = pl.BlockSpec(memory_space=pltpu.SMEM)
 VMEM = pl.BlockSpec(memory_space=pltpu.VMEM)
@@ -108,12 +113,11 @@
             rows = jnp.dot(
                 select, block[part * LANES : (part + 1) * LANES, :], preferred_element_type=F32
             )
+            if part == 1:
+                rows *= weight
             out_ref[:, b, :, part * width : (part + 1) * width] = rows.reshape(
                 PEERS, CAP, width
             ).astype(BF)
-        out_ref[:, b, :, 2 * width :] = (
-            jnp.broadcast_to(weight, (SLOTS, LANES)).reshape(PEERS, CAP, LANES).astype(BF)
-        )
 
 
 def build(z_me, blocks, topk):
@@ -122,19 +126,18 @@
     return pl.pallas_call(
         functools.partial(build_kernel, topk, count),
         in_specs=[SMEM] + [VMEM] * count,
-        out_shape=jax.ShapeDtypeStruct((PEERS, count, CAP, 2 * width + LANES), BF),
+        out_shape=jax.ShapeDtypeStruct((PEERS, count, CAP, 2 * width), BF),
         compiler_params=params(),
         name="build",
     )(z_me, *blocks)
 
 
 def expert_kernel(carried, rows_ref, wg_ref, wu_ref, wd_ref, *refs):
-    back_ref, x_ref, sc_ref, dg_ref, du_ref = refs[carried:]
+    *back_refs, x_ref, sc_ref, dg_ref, du_ref = refs[carried:]
     width = wg_ref.shape[0]
     rows = rows_ref[...]
-    x_ref[...] = rows[:, 0 : 2 * width]
-    x, g = rows[:, 0:width], rows[:, width : 2 * width]
-    weight = rows[:, 2 * width : 2 * width + 1].astype(F32)
+    x_ref[...] = rows
+    x, g = rows[:, 0:width], rows[:, width:]
     last = (((1,), (1,)), ((), ()))
     gate = jnp.dot(x, wg_ref[...], preferred_element_type=F32)
     up = jnp.dot(x, wu_ref[...], preferred_element_type=F32)
@@ -143,49 +146,71 @@
     active = gate * sigma
     hidden = active * up
     weight_grad = jnp.sum(back * hidden, axis=1, keepdims=True)
-    sc_ref[...] = (weight * hidden).astype(BF)
-    d_back = weight * back
-    d_gate = (d_back * up * sigma * (1.0 + gate * (1.0 - sigma))).astype(BF)
-    d_up = (d_back * active).astype(BF)
+    sc_ref[...] = hidden.astype(BF)
+    d_gate = (back * up * sigma * (1.0 + gate * (1.0 - sigma))).astype(BF)
+    d_up = (back * active).astype(BF)
     dg_ref[...] = d_gate
     du_ref[...] = d_up
     contrib = lax.dot_general(d_gate, wg_ref[...], last, preferred_element_type=F32)
     contrib += lax.dot_general(d_up, wu_ref[...], last, preferred_element_type=F32)
-    peers, count, cap, _ = back_ref.shape
-    back_ref[:, :, :, 0:width] = contrib.reshape(peers, count, cap, width).astype(BF)
+    blocks = rows.shape[0] // SLOTS
+    contrib = contrib.reshape(PEERS, blocks, CAP, width)
     weight_grad = jnp.broadcast_to(weight_grad, (rows.shape[0], LANES))
-    back_ref[:, :, :, width:] = weight_grad.reshape(peers, count, cap, LANES).astype(BF)
-
-
-def expert(rows, wg, wu, wd, kept, start, total):
+    weight_grad = weight_grad.reshape(PEERS, blocks, CAP, LANES)
+    at = 0
+    for ref in back_refs:
+        n = ref.shape[1]
+        ref[:, :, :, 0:width] = contrib[:, at : at + n].astype(BF)
+        ref[:, :, :, width:] = weight_grad[:, at : at + n].astype(BF)
+        at += n
+
+
+def expert(rows, wg, wu, wd, kept, start, backs, targets):
     width, hidden = wg.shape
     count = rows.shape[0]
     full = lambda a: pl.BlockSpec(a.shape, lambda i: (0, 0))
-    rows_at = lambda n: pl.BlockSpec((count, n), lambda i: (start // count, 0))
+    rows_at = lambda n: pl.BlockSpec((count, n), lambda i: (start * SLOTS // count, 0))
+
+    def back_spec(n, place):
+        return pl.BlockSpec((PEERS, n, CAP, width + LANES), lambda i: (0, place // n, 0, 0))
+
     kept_widths = (2 * width, hidden, hidden, hidden)
-    back_shape = (PEERS, count // SLOTS, CAP, width + LANES)
-    return pl.pallas_call(
-        functools.partial(expert_kernel, len(kept)),
+    carried = [(backs[w], o) for o, (w, _, _) in enumerate(targets) if w in backs]
+    carried += [(k, len(targets) + i) for i, k in enumerate(kept)]
+    return pl.pallas_call(
+        functools.partial(expert_kernel, len(carried)),
         grid=(1,),
         in_specs=[full(rows), full(wg), full(wu), full(wd)]
-        + [pl.BlockSpec(memory_space=pl.ANY)] * len(kept),
-        out_specs=[pl.BlockSpec(back_shape, lambda i: (0, 0, 0, 0))]
+        + [pl.BlockSpec(memory_space=pl.ANY)] * len(carried),
+        out_specs=[back_spec(n, place) for _, place, n in targets]
         + [rows_at(n) for n in kept_widths],
-        out_shape=[jax.ShapeDtypeStruct(back_shape, BF)]
-        + [jax.ShapeDtypeStruct((total, n), BF) for n in kept_widths],
-        input_output_aliases={4 + i: 1 + i for i in range(len(kept))},
+        out_shape=[
+            jax.ShapeDtypeStruct((PEERS, len(RETURNS[w]), CAP, width + LANES), BF)
+            for w, _, _ in targets
+        ]
+        + [jax.ShapeDtypeStruct((Z * SLOTS, n), BF) for n in kept_widths],
+        input_output_aliases={4 + i: o for i, (_, o) in enumerate(carried)},
         compiler_params=params(),
         name="expert",
-    )(rows, wg, wu, wd, *kept)
-
-
-def weights_kernel(rep_ref, x_ref, g_ref, sc_ref, dg_ref, du_ref, *refs):
-    keep_g, send_g, keep_u, send_u, keep_d, send_d, down_acc = refs
+    )(rows, wg, wu, wd, *[a for a, _ in carried])
+
+
+FIRST = (((0,), (0,)), ((), ()))
+
+
+def down_kernel(rep_ref, g_ref, sc_ref, keep_ref, send_ref, acc_ref):
+    acc_ref[...] = lax.dot_general(sc_ref[...], g_ref[...], FIRST, preferred_element_type=F32)
+    half, rep = keep_ref.shape[0], rep_ref[0]
+    keep_ref[...] = acc_ref[pl.ds(pl.multiple_of(rep * half, half), half), :].astype(BF)
+    send_ref[...] = acc_ref[pl.ds(pl.multiple_of((1 - rep) * half, half), half), :].astype(BF)
+
+
+def gate_up_kernel(rep_ref, x_ref, dg_ref, du_ref, *outs):
+    keep_g, send_g, keep_u, send_u = outs
     step, half_steps = pl.program_id(0), pl.num_programs(0) // 2
-    first = (((0,), (0,)), ((), ()))
     x = x_ref[...]
-    gate = lax.dot_general(x, dg_ref[...], first, preferred_element_type=F32).astype(BF)
-    up = lax.dot_general(x, du_ref[...], first, preferred_element_type=F32).astype(BF)
+    gate = lax.dot_general(x, dg_ref[...], FIRST, preferred_element_type=F32).astype(BF)
+    up = lax.dot_general(x, du_ref[...], FIRST, preferred_element_type=F32).astype(BF)
 
     @pl.when(step < half_steps)
     def _():
@@ -197,50 +222,58 @@
         keep_g[...] = gate
         keep_u[...] = up
 
-    down_acc[...] = lax.dot_general(
-        sc_ref[...], g_ref[...], first, preferred_element_type=F32
-    )
-    half = keep_d.shape[0]
-    rep = rep_ref[0]
-    keep_d[...] = down_acc[pl.ds(pl.multiple_of(rep * half, half), half), :].astype(BF)
-    send_d[...] = down_acc[pl.ds(pl.multiple_of((1 - rep) * half, half), half), :].astype(BF)
-
-
-def weights(rep, rows, sc, dg, du):
+
+def weights_down(rep, rows, sc):
     total, hidden = sc.shape
     width = rows.shape[1] // 2
     tile = 512
     steps = width // tile
-    half = steps // 2
-
-    def chosen(i, rep):
-        return lax.rem(i + (1 - rep[0]) * half, steps)
-
-    whole = pl.BlockSpec((total, hidden), lambda i, rep: (0, 0), pipeline_mode=pl.Buffered(1))
-    keep = pl.BlockSpec((tile, hidden), lambda i, rep: (jnp.maximum(i - half, 0), 0))
-    send = pl.BlockSpec((tile, hidden), lambda i, rep: (jnp.minimum(i, half - 1), 0))
     down = pl.BlockSpec((hidden // 2, tile), lambda i, rep: (0, i))
-    gu_shape = jax.ShapeDtypeStruct((width // 2, hidden), BF)
-    down_shape = jax.ShapeDtypeStruct((hidden // 2, width), BF)
-    return pl.pallas_call(
-        weights_kernel,
+    return pl.pallas_call(
+        down_kernel,
         grid_spec=pltpu.PrefetchScalarGridSpec(
             num_scalar_prefetch=1,
             grid=(steps,),
             in_specs=[
-                pl.BlockSpec((total, tile), lambda i, rep: (0, chosen(i, rep))),
                 pl.BlockSpec((total, tile), lambda i, rep: (0, steps + i)),
-                whole,
+                pl.BlockSpec((total, hidden), lambda i, rep: (0, 0)),
+            ],
+            out_specs=[down, down],
+            scratch_shapes=[pltpu.VMEM((hidden, tile), F32)],
+        ),
+        out_shape=[jax.ShapeDtypeStruct((hidden // 2, width), BF)] * 2,
+        compiler_params=params(),
+        name="weights_down",
+    )(rep, rows, sc)
+
+
+def weights_gate_up(rep, rows, dg, du):
+    total, hidden = dg.shape
+    width = rows.shape[1] // 2
+    tile = 512
+    steps = width // tile
+    half = steps // 2
+    whole = pl.BlockSpec((total, hidden), lambda i, rep: (0, 0))
+    keep = pl.BlockSpec((tile, hidden), lambda i, rep: (jnp.maximum(i - half, 0), 0))
+    send = pl.BlockSpec((tile, hidden), lambda i, rep: (jnp.minimum(i, half - 1), 0))
+    return pl.pallas_call(
+        gate_up_kernel,
+        grid_spec=pltpu.PrefetchScalarGridSpec(
+            num_scalar_prefetch=1,
+            grid=(steps,),
+            in_specs=[
+                pl.BlockSpec(
+                    (total, tile), lambda i, rep: (0, lax.rem(i + (1 - rep[0]) * half, steps))
+                ),
                 whole,
                 whole,
             ],
-            out_specs=[keep, send, keep, send, down, down],
-            scratch_shapes=[pltpu.VMEM((hidden, tile), F32)],
+            out_specs=[keep, send, keep, send],
         ),
-        out_shape=[gu_shape] * 4 + [down_shape] * 2,
-        compiler_params=params(),
-        name="weights",
-    )(rep, rows, rows, sc, dg, du)
+        out_shape=[jax.ShapeDtypeStruct((width // 2, hidden), BF)] * 4,
+        compiler_params=params(),
+        name="weights_gate_up",
+    )(rep, rows, dg, du)
 
 
 def combine_kernel(topk, count, z_ref, back_ref, *refs):
@@ -256,7 +289,11 @@
         )
         out_ref[0:LANES, :] = part.astype(out_ref.dtype)
         value = back_ref[:, b, :, width:].astype(F32).reshape(SLOTS, LANES)
-        grads = [jnp.sum(jnp.where(h, value, 0.0), axis=0, keepdims=True) for h in hits]
+        grads = [
+            jnp.sum(jnp.where(h, value, 0.0), axis=0, keepdims=True)
+            / meta[k : k + 1, 2 * LANES :]
+            for k, h in enumerate(hits)
+        ]
         grads.append(jnp.zeros((META - topk, LANES), F32))
         grads = jnp.concatenate(grads, axis=0)
         grads = jnp.concatenate([grads, jnp.zeros((META, width - LANES), F32)], axis=1)
@@ -299,24 +336,25 @@
             if name not in blocks and name != f"b{FAR}":
                 blocks[name] = z_shift(blocks[f"{kind}{s - 1}"], 1)
 
-    kept, backs = [], []
-    starts = (6 * SLOTS, 3 * SLOTS, 0)
-    for i, group in enumerate(ROUNDS):
+    kept, backs = [], {}
+    for group, start, targets in ROUNDS:
         sent = build(z_me, [blocks[r] for r in group], topk)
         rows = plane_exchange(sent)
         rows = rows.reshape(-1, rows.shape[-1])
-        back, *kept = expert(rows, wg, wu, wd, kept, starts[i], Z * SLOTS)
-        backs.append(back)
-    halves = weights(rep, *kept)
+        done = expert(rows, wg, wu, wd, kept, start, backs, targets)
+        kept = done[len(targets) :]
+        backs.update(zip((w for w, _, _ in targets), done))
+    rows, sc, dg, du = kept
+    halves = weights_down(rep, rows, sc)
+    halves = (*weights_gate_up(rep, rows, dg, du), *halves)
     grads = []
     for name, keep, send in zip(("gate", "up", "down"), halves[0::2], halves[1::2]):
         got = swap(send, "rep")
         grads.append((keep.astype(F32) + got.astype(F32)).astype(BF)[None])
 
     partial = {}
-    for i in range(len(ROUNDS) - 1, -1, -1):
+    for i, group in enumerate(RETURNS):
         returned = plane_exchange(backs[i])
-        group = ROUNDS[i]
         kinds = [F32 if r == "a0" else BF for r in group]
         parts = combine(z_me, returned, [blocks[r] for r in group], topk, kinds)
         partial.update(zip(group, parts))

time: 316 us -> 320 us (1.013)
  Pallas kernels: 60.9 us -> 65.2 us
    pallas_call x4 -> x5, Pallas kernels: 36.6 us -> 41.1 us  [the longest x3 27 us: expert(): pl.pallas_call(functools.partial(expert_kernel, len(carried)), grid=(1,),...]
    ppermute x14, starting transfers between devices: 18.2 us -> 14.6 us  [z_shift(): return lax.ppermute(value, ('z', 'c'), pairs)]
    ppermute x14, waiting for transfers between devices: 77 us -> 80.2 us  [z_shift(): return lax.ppermute(value, ('z', 'c'), pairs)]
  transfers between devices with their start and end apart: 23 -> 23, of which waited for: 13 -> 10; matrix products, arithmetic and copies ran while one was open for 3% -> 3% of each run, Pallas kernels for 19% -> 20%
where the time goes in v1:
time: 320 us; the launch traced here: 319 us
  waiting for transfers between devices  148 us (46%)
  Pallas kernels  65.2 us (20%)
  starting transfers between devices  59.2 us (18%)
  blocking collectives  31.5 us (10%)
  other arithmetic  12.2 us (4%)
    ppermute x14, waiting for transfers between devices, z_shift(): return lax.ppermute(value, ('z', 'c'), pairs)  80.2 us
    all_to_all x5, starting transfers between devices, plane_exchange(): return lax.all_to_all(value, PLANE, split_axis=0, concat_axis=0, tiled=True)  39.5 us
    all_to_all x5, waiting for transfers between devices, plane_exchange(): return lax.all_to_all(value, PLANE, split_axis=0, concat_axis=0, tiled=True)  34.1 us
    ppermute x4, waiting for transfers between devices, swap(): return lax.ppermute(value, axis, [(0, 1), (1, 0)])  33.4 us
    all_to_all x1, blocking collectives, plane_exchange(): return lax.all_to_all(value, PLANE, split_axis=0, concat_axis=0, tiled=True)  31.5 us
    pallas_call x3, Pallas kernels, expert(): pl.pallas_call(functools.partial(expert_kernel, len(carried)), grid=(1,),...  27 us
    ppermute x14, starting transfers between devices, z_shift(): return lax.ppermute(value, ('z', 'c'), pairs)  14.6 us
    pallas_call x3, Pallas kernels, build(): pl.pallas_call(functools.partial(build_kernel, topk, count), in_specs=[SM...  12.8 us
  transfers between devices with their start and end apart: 23, of which 10 were waited for; matrix products, arithmetic and copies ran while one was open for 3% of the time, Pallas kernels for 20%

profile of v1, /device:TPU:1, one launch (start us, length us, event | category | flops | bytes accessed | tf_op | source)
XLA Modules:
  0.0 319.0 jit_solution(4916638134552156057)
XLA Ops:
  0.6 2.4 pack.1.refs_0_
  3.0 3.2 %collective-permute-start.1 = (bf16[264,2048]{1,0:T(8,128)(2,1)}, bf16[264,2048]{1,0:T(8,128)(2,1)}, u32[]{:S(2)}, u32[]{:S(2)}) collective-permute-start(bf16[264,2048]{1,0:T(8,128)(2,1)} %pack.1.refs_0_), channel_id=1, source_target_pairs={{0,1},{1,0},{2,3},{3,2},{4,5},{5,4},{6,7},{7,6},{8,9},{9,8},{10,11... | collective-permute-start | bytes 3244040 | tf_op jit(solution)/shard_map/ppermute | solution.py:44
  6.2 3.9 %collective-permute-start = (bf16[264,2048]{1,0:T(8,128)(2,1)}, bf16[264,2048]{1,0:T(8,128)(2,1)}, u32[]{:S(2)}, u32[]{:S(2)}) collective-permute-start(bf16[264,2048]{1,0:T(8,128)(2,1)} %pack.1.refs_0_), channel_id=1, source_target_pairs={{0,8},{1,57},{8,16},{9,1},{16,24},{17,9},{24,32},{25,17},{32,40},{... | collective-permute-start | bytes 3244040 | tf_op jit(solution)/shard_map/ppermute | solution.py:40
  10.1 2.7 collective-permute-start.2
  12.8 9.7 %collective-permute-done.refs_1_.refs_3_ = bf16[264,2048]{1,0:T(8,128)(2,1)} collective-permute-done((bf16[264,2048]{1,0:T(8,128)(2,1)}, bf16[264,2048]{1,0:T(8,128)(2,1)}, u32[]{:S(2)}, u32[]{:S(2)}) %collective-permute-start) | collective-permute-done | bytes 1081376 | tf_op jit(solution)/shard_map/ppermute | solution.py:40
  22.5 3.6 %build.3 = bf16[16,2,8,4096]{3,2,1,0:T(8,128)(2,1)} custom-call(s32[1]{0:T(128)} %bitcast.z_ref, bf16[264,2048]{1,0:T(8,128)(2,1)} %pack.1.refs_0_, bf16[264,2048]{1,0:T(8,128)(2,1)} %collective-permute-done.refs_1_.refs_3_), custom_call_target="tpu_custom_call" | custom-call | tf_op jit(solution)/shard_map/build/pallas_call | solution.py:126
  26.1 8.2 %all-to-all-start = ((bf16[16,2,8,4096]{3,2,1,0:T(8,128)(2,1)}), bf16[16,2,8,4096]{3,2,1,0:T(8,128)(2,1)}, u32[]{:S(2)}, u32[]{:S(2)}) async-start(bf16[16,2,8,4096]{3,2,1,0:T(8,128)(2,1)} %build.3), calls=%async_computation | async-start | bytes 4194304 | tf_op jit(solution)/shard_map/all_to_all | solution.py:320
  34.4 1.9 collective-permute-start.3
  36.3 0.9 collective-permute-start.4
  37.2 11.8 %collective-permute-done.3.refs_1_ = bf16[264,2048]{1,0:T(8,128)(2,1)} collective-permute-done((bf16[264,2048]{1,0:T(8,128)(2,1)}, bf16[264,2048]{1,0:T(8,128)(2,1)}, u32[]{:S(2)}, u32[]{:S(2)}) %collective-permute-start.3) | collective-permute-done | bytes 1081376 | tf_op jit(solution)/shard_map/ppermute | solution.py:40
  49.0 11.6 %collective-permute-done.4.refs_2_ = bf16[264,2048]{1,0:T(8,128)(2,1)} collective-permute-done((bf16[264,2048]{1,0:T(8,128)(2,1)}, bf16[264,2048]{1,0:T(8,128)(2,1)}, u32[]{:S(2)}, u32[]{:S(2)}) %collective-permute-start.4) | collective-permute-done | bytes 1081376 | tf_op jit(solution)/shard_map/ppermute | solution.py:40
  60.5 4.6 %build.4 = bf16[16,3,8,4096]{3,2,1,0:T(8,128)(2,1)} custom-call(s32[1]{0:T(128)} %bitcast.z_ref, bf16[264,2048]{1,0:T(8,128)(2,1)} %collective-permute-done.2.refs_0_, bf16[264,2048]{1,0:T(8,128)(2,1)} %collective-permute-done.3.refs_1_, bf16[264,2048]{1,0:T(8,128)(2,1)} %collective-permute-done.4.refs_2_), custom_call_target="tpu_custom_call" | custom-call | tf_op jit(solution)/shard_map/build/pallas_call | solution.py:126
  65.1 9.3 %all-to-all-start.2 = ((bf16[16,3,8,4096]{3,2,1,0:T(8,128)(2,1)}), bf16[16,3,8,4096]{3,2,1,0:T(8,128)(2,1)}, u32[]{:S(2)}, u32[]{:S(2)}) async-start(bf16[16,3,8,4096]{3,2,1,0:T(8,128)(2,1)} %build.4), calls=%async_computation.2 | async-start | bytes 6291456 | tf_op jit(solution)/shard_map/all_to_all | solution.py:320
  74.4 0.7 collective-permute-start.5
  75.2 13.9 %collective-permute-done.5.refs_0_ = bf16[264,2048]{1,0:T(8,128)(2,1)S(1)} collective-permute-done((bf16[264,2048]{1,0:T(8,128)(2,1)}, bf16[264,2048]{1,0:T(8,128)(2,1)S(1)}, u32[]{:S(2)}, u32[]{:S(2)}) %collective-permute-start.5) | collective-permute-done | bytes 1081376 | tf_op jit(solution)/shard_map/ppermute | solution.py:40
  89.0 1.0 copy-done
  90.0 1.9 collective-permute-start.7
  92.0 12.4 %collective-permute-done.7.refs_2_ = bf16[264,2048]{1,0:T(8,128)(2,1)S(1)} collective-permute-done((bf16[264,2048]{1,0:T(8,128)(2,1)S(1)}, bf16[264,2048]{1,0:T(8,128)(2,1)S(1)}, u32[]{:S(2)}, u32[]{:S(2)}) %collective-permute-start.7) | collective-permute-done | bytes 1081376 | tf_op jit(solution)/shard_map/ppermute | solution.py:40
  104.4 1.0 copy-done.1
  105.4 10.6 %collective-permute-done.6.refs_1_ = bf16[264,2048]{1,0:T(8,128)(2,1)} collective-permute-done((bf16[264,2048]{1,0:T(8,128)(2,1)}, bf16[264,2048]{1,0:T(8,128)(2,1)}, u32[]{:S(2)}, u32[]{:S(2)}) %collective-permute-start.6) | collective-permute-done | bytes 1081376 | tf_op jit(solution)/shard_map/ppermute | solution.py:40
  116.0 4.6 %build.5 = bf16[16,3,8,4096]{3,2,1,0:T(8,128)(2,1)} custom-call(s32[1]{0:T(128)} %bitcast.z_ref, bf16[264,2048]{1,0:T(8,128)(2,1)} %copy-done, bf16[264,2048]{1,0:T(8,128)(2,1)} %collective-permute-done.6.refs_1_, bf16[264,2048]{1,0:T(8,128)(2,1)} %copy-done.1), custom_call_target="tpu_custom_call" | custom-call | tf_op jit(solution)/shard_map/build/pallas_call | solution.py:126
  120.6 11.2 %all-to-all-start.4 = ((bf16[16,3,8,4096]{3,2,1,0:T(8,128)(2,1)}), bf16[16,3,8,4096]{3,2,1,0:T(8,128)(2,1)}, u32[]{:S(2)}, u32[]{:S(2)}) async-start(bf16[16,3,8,4096]{3,2,1,0:T(8,128)(2,1)} %build.5), calls=%async_computation.4 | async-start | bytes 6291456 | tf_op jit(solution)/shard_map/all_to_all | solution.py:320
  131.8 7.8 %expert.3 = (bf16[16,1,8,2176]{3,2,1,0:T(8,128)(2,1)}, bf16[16,4,8,2176]{3,2,1,0:T(8,128)(2,1)}, bf16[1024,4096]{1,0:T(8,128)(2,1)}, bf16[1024,384]{1,0:T(8,128)...) custom-call(bf16[256,4096]{1,0:T(8,128)(2,1)} %bitcast.3.rows_ref, bf16[2048,384]{1,0:T(8,128)(2,1)} %bitcast.18, ...), custom_call_target="tpu_custom_call" | custom-call | tf_op jit(solution)/shard_map/expert/pallas_call | solution.py:180
  139.6 34.1 %all-to-all-done.4 = bf16[16,3,8,4096]{3,2,1,0:T(8,128)(2,1)} async-done(((bf16[16,3,8,4096]{3,2,1,0:T(8,128)(2,1)}), bf16[16,3,8,4096]{3,2,1,0:T(8,128)(2,1)}, u32[]{:S(2)}, u32[]{:S(2)}) %all-to-all-start.4) | async-done | bytes 3145760 | tf_op jit(solution)/shard_map/all_to_all | solution.py:320
  173.7 6.2 %all-to-all-start.1 = ((bf16[16,1,8,2176]{3,2,1,0:T(8,128)(2,1)}), bf16[16,1,8,2176]{3,2,1,0:T(8,128)(2,1)S(1)}, u32[]{:S(2)}, u32[]{:S(2)}) async-start(bf16[16,1,8,2176]{3,2,1,0:T(8,128)(2,1)} %get-tuple-element.34), calls=%async_computation.1 | async-start | bytes 1114112 | tf_op jit(solution)/shard_map/all_to_all | solution.py:320
  179.9 10.3 %expert.4 = (bf16[16,4,8,2176]{3,2,1,0:T(8,128)(2,1)}, bf16[1024,4096]{1,0:T(8,128)(2,1)}, bf16[1024,384]{1,0:T(8,128)(2,1)}, bf16[1024,384]{1,0:T(8,128)(2,1)}, bf16[1024,384]{1,0:T(8,128)(2,1)}) custom-call(bf16[384,4096]{1,0:T(8,128)(2,1)} %bitcast.7.rows_ref, ...), custom_call_target="tpu_custom_call", output_to_operand_aliasing={{0}: (4, {}), {1}: (5, {}), {2}: (6, {}), {3}: (7, {}), {4}... | custom-call | tf_op jit(solution)/shard_map/expert/pallas_call | solution.py:180
  190.1 9.0 %expert.5 = (bf16[16,3,8,2176]{3,2,1,0:T(8,128)(2,1)}, bf16[1024,4096]{1,0:T(8,128)(2,1)}, bf16[1024,384]{1,0:T(8,128)(2,1)}, bf16[1024,384]{1,0:T(8,128)(2,1)}, bf16[1024,384]{1,0:T(8,128)(2,1)}) custom-call(bf16[384,4096]{1,0:T(8,128)(2,1)} %bitcast.8.rows_ref, ...), custom_call_target="tpu_custom_call", output_to_operand_aliasing={{1}: (4, {}), {2}: (5, {}), {3}: (6, {}), {4}: (7, {})} | custom-call | tf_op jit(solution)/shard_map/expert/pallas_call | solution.py:180
  199.1 31.5 %all_to_all.30.back_ref = bf16[16,3,8,2176]{3,2,1,0:T(8,128)(2,1)} all-to-all(bf16[16,3,8,2176]{3,2,1,0:T(8,128)(2,1)} %get-tuple-element.47), channel_id=1, replica_groups=mesh['rep'=2,'yh'=2,'z'=8,'x'=4,'c'=2] {'yh','x','c'}, dimensions={0} | all-to-all | bytes 3342336 | tf_op jit(solution)/shard_map/all_to_all | solution.py:320
  230.6 4.6 %all-to-all-start.3 = ((bf16[16,4,8,2176]{3,2,1,0:T(8,128)(2,1)}), bf16[16,4,8,2176]{3,2,1,0:T(8,128)(2,1)}, u32[]{:S(2)}, u32[]{:S(2)}) async-start(bf16[16,4,8,2176]{3,2,1,0:T(8,128)(2,1)} %get-tuple-element.40), calls=%async_computation.3 | async-start | bytes 4456448 | tf_op jit(solution)/shard_map/all_to_all | solution.py:320
  235.2 3.1 combine.5
  238.2 10.2 %collective-permute-done.8 = bf16[136,2048]{1,0:T(8,128)(2,1)S(1)} collective-permute-done((bf16[136,2048]{1,0:T(8,128)(2,1)}, bf16[136,2048]{1,0:T(8,128)(2,1)S(1)}, u32[]{:S(2)}, u32[]{:S(2)}) %collective-permute-start.8) | collective-permute-done | bytes 557088 | tf_op jit(solution)/shard_map/ppermute | solution.py:40
  248.4 2.0 add_convert_fusion.7
  250.5 2.4 combine.3
  252.9 5.6 %weights_down.1 = (bf16[192,2048]{1,0:T(8,128)(2,1)}, bf16[192,2048]{1,0:T(8,128)(2,1)}) custom-call(s32[1]{0:T(128)} %bitcast.10.rep_ref, bf16[1024,4096]{1,0:T(8,128)(2,1)} %get-tuple-element.53.x_ref.g_ref, bf16[1024,384]{1,0:T(8,128)(2,1)} %get-tuple-element.60.sc_ref), custom_call_target="tpu_custom_call" | custom-call | tf_op jit(solution)/shard_map/weights_down/pallas_call | solution.py:232
  258.9 8.5 %weights_gate_up.1 = (bf16[1024,384]{1,0:T(8,128)(2,1)}, bf16[1024,384]{1,0:T(8,128)(2,1)}, bf16[1024,384]{1,0:T(8,128)(2,1)}, bf16[1024,384]{1,0:T(8,128)(2,1)}) custom-call(s32[1]{0:T(128)} %bitcast.10.rep_ref, bf16[1024,4096]{1,0:T(8,128)(2,1)} %get-tuple-element.53.x_ref.g_ref, bf16[1024,384]{1,0:T(8,128)(2,1)} %get-tuple-element.54.dg_ref, ...), custom_call_target="tpu_custom_call" | custom-call | tf_op jit(solution)/shard_map/weights_gate_up/pallas_call | solution.py:259
  267.4 1.1 collective-permute-start.16
  268.8 3.4 %combine.4 = (bf16[136,2048]{1,0:T(8,128)(2,1)}, bf16[136,2048]{1,0:T(8,128)(2,1)}, bf16[136,2048]{1,0:T(8,128)(2,1)}, bf16[136,2048]{1,0:T(8,128)(2,1)}) custom-call(s32[1]{0:T(128)} %bitcast.z_ref, bf16[16,4,8,2176]{3,2,1,0:T(8,128)(2,1)} %all-to-all-done.3.back_ref, bf16[264,2048]{1,0:T(8,128)(2,1)} %collective-permute-done.2.refs_0_, ...), custom_call_target="tpu_custom_call" | custom-call | tf_op jit(solution)/shard_map/combine/pallas_call | solution.py:307
  272.3 1.4 add_convert_fusion.4
  273.8 1.3 add_convert_fusion.6
  275.1 1.7 collective-permute-start.10
  276.8 20.1 %collective-permute-done.16 = bf16[1024,384]{1,0:T(8,128)(2,1)} collective-permute-done((bf16[1024,384]{1,0:T(8,128)(2,1)}, bf16[1024,384]{1,0:T(8,128)(2,1)}, u32[]{:S(2)}, u32[]{:S(2)}) %collective-permute-start.16) | collective-permute-done | bytes 786464 | tf_op jit(solution)/shard_map/ppermute | solution.py:44
  296.9 2.3 fusion.3
  299.4 0.6 collective-permute-start.14
  300.5 13.3 %collective-permute-done.15 = bf16[1024,384]{1,0:T(8,128)(2,1)} collective-permute-done((bf16[1024,384]{1,0:T(8,128)(2,1)}, bf16[1024,384]{1,0:T(8,128)(2,1)}, u32[]{:S(2)}, u32[]{:S(2)}) %collective-permute-start.15) | collective-permute-done | bytes 786464 | tf_op jit(solution)/shard_map/ppermute | solution.py:44
  313.8 2.3 fusion.2
  316.1 1.2 fusion.4
  317.4 0.6 fusion.7
  318.0 1.0 fusion.1
  (41 shorter events, 1.7 us)
Async XLA Ops:
  3.0 7.1 %collective-permute-start.1 = (bf16[264,2048]{1,0:T(8,128)(2,1)}, bf16[264,2048]{1,0:T(8,128)(2,1)}, u32[]{:S(2)}, u32[]{:S(2)}) collective-permute-start(bf16[264,2048]{1,0:T(8,128)(2,1)} %pack.1.refs_0_), channel_id=1, source_target_pairs={{0,1},{1,0},{2,3},{3,2},{4,5},{5,4},{6,7},{7,6},{8,9},{9,8},{10,11... | collective-permute-start | bytes 3244040 | tf_op jit(solution)/shard_map/ppermute | solution.py:44
  6.2 16.3 %collective-permute-start = (bf16[264,2048]{1,0:T(8,128)(2,1)}, bf16[264,2048]{1,0:T(8,128)(2,1)}, u32[]{:S(2)}, u32[]{:S(2)}) collective-permute-start(bf16[264,2048]{1,0:T(8,128)(2,1)} %pack.1.refs_0_), channel_id=1, source_target_pairs={{0,8},{1,57},{8,16},{9,1},{16,24},{17,9},{24,32},{25,17},{32,40},{... | collective-permute-start | bytes 3244040 | tf_op jit(solution)/shard_map/ppermute | solution.py:40
  10.1 26.2 %collective-permute-start.2 = (bf16[264,2048]{1,0:T(8,128)(2,1)}, bf16[264,2048]{1,0:T(8,128)(2,1)}, u32[]{:S(2)}, u32[]{:S(2)}) collective-permute-start(bf16[264,2048]{1,0:T(8,128)(2,1)} %collective-permute-done.1), channel_id=1, source_target_pairs={{0,8},{1,57},{8,16},{9,1},{16,24},{17,9},{24,32},{25,17},{32,40},{... | collective-permute-start | bytes 3244040 | tf_op jit(solution)/shard_map/ppermute | solution.py:40
  26.1 39.0 %all-to-all-start = ((bf16[16,2,8,4096]{3,2,1,0:T(8,128)(2,1)}), bf16[16,2,8,4096]{3,2,1,0:T(8,128)(2,1)}, u32[]{:S(2)}, u32[]{:S(2)}) async-start(bf16[16,2,8,4096]{3,2,1,0:T(8,128)(2,1)} %build.3), calls=%async_computation | async-start | bytes 4194304 | tf_op jit(solution)/shard_map/all_to_all | solution.py:320
  34.4 14.6 %collective-permute-start.3 = (bf16[264,2048]{1,0:T(8,128)(2,1)}, bf16[264,2048]{1,0:T(8,128)(2,1)}, u32[]{:S(2)}, u32[]{:S(2)}) collective-permute-start(bf16[264,2048]{1,0:T(8,128)(2,1)} %collective-permute-done.refs_1_.refs_3_), channel_id=1, source_target_pairs={{0,8},{1,57},{8,16},{9,1},{16,24},{17,9},{24,32},{25,17},{32,40},{... | collective-permute-start | bytes 3244040 | tf_op jit(solution)/shard_map/ppermute | solution.py:40
  36.3 24.3 %collective-permute-start.4 = (bf16[264,2048]{1,0:T(8,128)(2,1)}, bf16[264,2048]{1,0:T(8,128)(2,1)}, u32[]{:S(2)}, u32[]{:S(2)}) collective-permute-start(bf16[264,2048]{1,0:T(8,128)(2,1)} %collective-permute-done.2.refs_0_), channel_id=1, source_target_pairs={{0,8},{1,57},{8,16},{9,1},{16,24},{17,9},{24,32},{25,17},{32,40},{... | collective-permute-start | bytes 3244040 | tf_op jit(solution)/shard_map/ppermute | solution.py:40
  65.1 55.5 %all-to-all-start.2 = ((bf16[16,3,8,4096]{3,2,1,0:T(8,128)(2,1)}), bf16[16,3,8,4096]{3,2,1,0:T(8,128)(2,1)}, u32[]{:S(2)}, u32[]{:S(2)}) async-start(bf16[16,3,8,4096]{3,2,1,0:T(8,128)(2,1)} %build.4), calls=%async_computation.2 | async-start | bytes 6291456 | tf_op jit(solution)/shard_map/all_to_all | solution.py:320
  74.4 14.6 %collective-permute-start.5 = (bf16[264,2048]{1,0:T(8,128)(2,1)}, bf16[264,2048]{1,0:T(8,128)(2,1)S(1)}, u32[]{:S(2)}, u32[]{:S(2)}) collective-permute-start(bf16[264,2048]{1,0:T(8,128)(2,1)} %collective-permute-done.3.refs_1_), channel_id=1, source_target_pairs={{0,8},{1,57},{8,16},{9,1},{16,24},{17,9},{24,32},{25,17},{32,40},{... | collective-permute-start | bytes 3244040 | tf_op jit(solution)/shard_map/ppermute | solution.py:40
  89.0 1.0 copy-start
  90.0 14.4 %collective-permute-start.7 = (bf16[264,2048]{1,0:T(8,128)(2,1)S(1)}, bf16[264,2048]{1,0:T(8,128)(2,1)S(1)}, u32[]{:S(2)}, u32[]{:S(2)}) collective-permute-start(bf16[264,2048]{1,0:T(8,128)(2,1)S(1)} %collective-permute-done.5.refs_0_), channel_id=1, source_target_pairs={{0,8},{1,57},{8,16},{9,1},{16,24},{17,9},{24,32},{25,17},{32,40},{... | collective-permute-start | bytes 3244040 | tf_op jit(solution)/shard_map/ppermute | solution.py:40
  92.0 24.1 %collective-permute-start.6 = (bf16[264,2048]{1,0:T(8,128)(2,1)}, bf16[264,2048]{1,0:T(8,128)(2,1)}, u32[]{:S(2)}, u32[]{:S(2)}) collective-permute-start(bf16[264,2048]{1,0:T(8,128)(2,1)} %collective-permute-done.4.refs_2_), channel_id=1, source_target_pairs={{0,8},{1,57},{8,16},{9,1},{16,24},{17,9},{24,32},{25,17},{32,40},{... | collective-permute-start | bytes 3244040 | tf_op jit(solution)/shard_map/ppermute | solution.py:40
  104.4 1.0 copy-start.1
  120.6 53.1 %all-to-all-start.4 = ((bf16[16,3,8,4096]{3,2,1,0:T(8,128)(2,1)}), bf16[16,3,8,4096]{3,2,1,0:T(8,128)(2,1)}, u32[]{:S(2)}, u32[]{:S(2)}) async-start(bf16[16,3,8,4096]{3,2,1,0:T(8,128)(2,1)} %build.5), calls=%async_computation.4 | async-start | bytes 6291456 | tf_op jit(solution)/shard_map/all_to_all | solution.py:320
  173.7 25.4 %all-to-all-start.1 = ((bf16[16,1,8,2176]{3,2,1,0:T(8,128)(2,1)}), bf16[16,1,8,2176]{3,2,1,0:T(8,128)(2,1)S(1)}, u32[]{:S(2)}, u32[]{:S(2)}) async-start(bf16[16,1,8,2176]{3,2,1,0:T(8,128)(2,1)} %get-tuple-element.34), calls=%async_computation.1 | async-start | bytes 1114112 | tf_op jit(solution)/shard_map/all_to_all | solution.py:320
  199.1 31.5 %copy-start.3 = (bf16[16,1,8,2176]{3,2,1,0:T(8,128)(2,1)}, bf16[16,1,8,2176]{3,2,1,0:T(8,128)(2,1)S(1)}, u32[]{:S(2)}) copy-start(bf16[16,1,8,2176]{3,2,1,0:T(8,128)(2,1)S(1)} %all-to-all-done.1.back_ref) | copy-start | bytes 1671172
  230.6 38.2 %all-to-all-start.3 = ((bf16[16,4,8,2176]{3,2,1,0:T(8,128)(2,1)}), bf16[16,4,8,2176]{3,2,1,0:T(8,128)(2,1)}, u32[]{:S(2)}, u32[]{:S(2)}) async-start(bf16[16,4,8,2176]{3,2,1,0:T(8,128)(2,1)} %get-tuple-element.40), calls=%async_computation.3 | async-start | bytes 4456448 | tf_op jit(solution)/shard_map/all_to_all | solution.py:320
  238.2 10.2 %collective-permute-start.8 = (bf16[136,2048]{1,0:T(8,128)(2,1)}, bf16[136,2048]{1,0:T(8,128)(2,1)S(1)}, u32[]{:S(2)}, u32[]{:S(2)}) collective-permute-start(bf16[136,2048]{1,0:T(8,128)(2,1)} %get-tuple-element.49), channel_id=1, source_target_pairs={{0,56},{1,9},{8,0},{9,17},{16,8},{17,25},{24,16},{25,33},{32,24},{... | collective-permute-start | bytes 1671176 | tf_op jit(solution)/shard_map/ppermute | solution.py:40
  238.2 34.0 %collective-permute-start.12 = (bf16[136,2048]{1,0:T(8,128)(2,1)}, bf16[136,2048]{1,0:T(8,128)(2,1)}, u32[]{:S(2)}, u32[]{:S(2)}) collective-permute-start(bf16[136,2048]{1,0:T(8,128)(2,1)} %get-tuple-element.52), channel_id=1, source_target_pairs={{0,56},{1,9},{8,0},{9,17},{16,8},{17,25},{24,16},{25,33},{32,24},{... | collective-permute-start | bytes 1671176 | tf_op jit(solution)/shard_map/ppermute | solution.py:40
  250.4 23.4 %collective-permute-start.9 = (bf16[136,2048]{1,0:T(8,128)(2,1)}, bf16[136,2048]{1,0:T(8,128)(2,1)}, u32[]{:S(2)}, u32[]{:S(2)}) collective-permute-start(bf16[136,2048]{1,0:T(8,128)(2,1)} %add_convert_fusion.7), channel_id=1, source_target_pairs={{0,56},{1,9},{8,0},{9,17},{16,8},{17,25},{24,16},{25,33},{32,24},{... | collective-permute-start | bytes 1671176 | tf_op jit(solution)/shard_map/ppermute | solution.py:40
  258.5 57.6 %collective-permute-start.17 = (bf16[192,2048]{1,0:T(8,128)(2,1)}, bf16[192,2048]{1,0:T(8,128)(2,1)S(1)}, u32[]{:S(2)}, u32[]{:S(2)}) collective-permute-start(bf16[192,2048]{1,0:T(8,128)(2,1)} %get-tuple-element.62), channel_id=1, source_target_pairs={{0,128},{128,0},{1,129},{129,1},{2,130},{130,2},{3,131},{131,3},{4... | collective-permute-start | bytes 2359304 | tf_op jit(solution)/shard_map/ppermute | solution.py:44
  267.4 29.6 %collective-permute-start.16 = (bf16[1024,384]{1,0:T(8,128)(2,1)}, bf16[1024,384]{1,0:T(8,128)(2,1)}, u32[]{:S(2)}, u32[]{:S(2)}) collective-permute-start(bf16[1024,384]{1,0:T(8,128)(2,1)} %get-tuple-element.59), channel_id=1, source_target_pairs={{0,128},{128,0},{1,129},{129,1},{2,130},{130,2},{3,131},{131,3},{4... | collective-permute-start | bytes 2359304 | tf_op jit(solution)/shard_map/ppermute | solution.py:44
  268.4 45.4 %collective-permute-start.15 = (bf16[1024,384]{1,0:T(8,128)(2,1)}, bf16[1024,384]{1,0:T(8,128)(2,1)}, u32[]{:S(2)}, u32[]{:S(2)}) collective-permute-start(bf16[1024,384]{1,0:T(8,128)(2,1)} %get-tuple-element.57), channel_id=1, source_target_pairs={{0,128},{128,0},{1,129},{129,1},{2,130},{130,2},{3,131},{131,3},{4... | collective-permute-start | bytes 2359304 | tf_op jit(solution)/shard_map/ppermute | solution.py:44
  272.3 1.5 copy-start.9
  273.7 23.2 %copy-start.6 = (bf16[1024,384]{1,0:T(8,128)(2,1)S(1)}, bf16[1024,384]{1,0:T(8,128)(2,1)}, u32[]{:S(2)}) copy-start(bf16[1024,384]{1,0:T(8,128)(2,1)} %get-tuple-element.58) | copy-start | bytes 2359300
  273.7 25.5 %collective-permute-start.13 = (bf16[136,2048]{1,0:T(8,128)(2,1)S(1)}, bf16[136,2048]{1,0:T(8,128)(2,1)S(1)}, u32[]{:S(2)}, u32[]{:S(2)}) collective-permute-start(bf16[136,2048]{1,0:T(8,128)(2,1)S(1)} %add_convert_fusion.4), channel_id=1, source_target_pairs={{0,56},{1,9},{8,0},{9,17},{16,8},{17,25},{24,16},{25,33},{32,24},{... | collective-permute-start | bytes 1671176 | tf_op jit(solution)/shard_map/ppermute | solution.py:40
  275.1 24.9 %collective-permute-start.10 = (bf16[136,2048]{1,0:T(8,128)(2,1)S(1)}, bf16[136,2048]{1,0:T(8,128)(2,1)S(1)}, u32[]{:S(2)}, u32[]{:S(2)}) collective-permute-start(bf16[136,2048]{1,0:T(8,128)(2,1)S(1)} %add_convert_fusion.6), channel_id=1, source_target_pairs={{0,56},{1,9},{8,0},{9,17},{16,8},{17,25},{24,16},{25,33},{32,24},{... | collective-permute-start | bytes 1671176 | tf_op jit(solution)/shard_map/ppermute | solution.py:40
  296.9 2.3 copy-start.8
  299.2 1.1 copy-start.7
  299.4 14.4 %copy-start.5 = (bf16[1024,384]{1,0:T(8,128)(2,1)S(1)}, bf16[1024,384]{1,0:T(8,128)(2,1)}, u32[]{:S(2)}) copy-start(bf16[1024,384]{1,0:T(8,128)(2,1)} %get-tuple-element.56) | copy-start | bytes 2359300
  299.4 17.9 %collective-permute-start.14 = (bf16[136,2048]{1,0:T(8,128)(2,1)S(1)}, bf16[136,2048]{1,0:T(8,128)(2,1)S(1)}, u32[]{:S(2)}, u32[]{:S(2)}) collective-permute-start(bf16[136,2048]{1,0:T(8,128)(2,1)S(1)} %add_convert_fusion.3), channel_id=1, source_target_pairs={{0,57},{1,8},{8,1},{9,16},{16,9},{17,24},{24,17},{25,32},{32,25},{... | collective-permute-start | bytes 1671176 | tf_op jit(solution)/shard_map/ppermute | solution.py:40
  300.4 16.8 %collective-permute-start.11 = (bf16[136,2048]{1,0:T(8,128)(2,1)S(1)}, bf16[136,2048]{1,0:T(8,128)(2,1)S(1)}, u32[]{:S(2)}, u32[]{:S(2)}) collective-permute-start(bf16[136,2048]{1,0:T(8,128)(2,1)S(1)} %add_convert_fusion.5), channel_id=1, source_target_pairs={{0,56},{1,9},{8,0},{9,17},{16,8},{17,25},{24,16},{25,33},{32,24},{... | collective-permute-start | bytes 1671176 | tf_op jit(solution)/shard_map/ppermute | solution.py:40
  313.8 2.3 copy-start.4
  316.1 1.3 copy-start.2

commit v2 on v1

--- a/solution.py
+++ b/solution.py
@@ -113,11 +113,12 @@
             rows = jnp.dot(
                 select, block[part * LANES : (part + 1) * LANES, :], preferred_element_type=F32
             )
-            if part == 1:
-                rows *= weight
             out_ref[:, b, :, part * width : (part + 1) * width] = rows.reshape(
                 PEERS, CAP, width
             ).astype(BF)
+        out_ref[:, b, :, 2 * width :] = (
+            jnp.broadcast_to(weight, (SLOTS, LANES)).reshape(PEERS, CAP, LANES).astype(BF)
+        )
 
 
 def build(z_me, blocks, topk):
@@ -126,7 +127,7 @@
     return pl.pallas_call(
         functools.partial(build_kernel, topk, count),
         in_specs=[SMEM] + [VMEM] * count,
-        out_shape=jax.ShapeDtypeStruct((PEERS, count, CAP, 2 * width), BF),
+        out_shape=jax.ShapeDtypeStruct((PEERS, count, CAP, 2 * width + LANES), BF),
         compiler_params=params(),
         name="build",
     )(z_me, *blocks)
@@ -136,8 +137,9 @@
     *back_refs, x_ref, sc_ref, dg_ref, du_ref = refs[carried:]
     width = wg_ref.shape[0]
     rows = rows_ref[...]
-    x_ref[...] = rows
-    x, g = rows[:, 0:width], rows[:, width:]
+    x_ref[...] = rows[:, 0 : 2 * width]
+    x, g = rows[:, 0:width], rows[:, width : 2 * width]
+    weight = rows[:, 2 * width : 2 * width + 1].astype(F32)
     last = (((1,), (1,)), ((), ()))
     gate = jnp.dot(x, wg_ref[...], preferred_element_type=F32)
     up = jnp.dot(x, wu_ref[...], preferred_element_type=F32)
@@ -146,9 +148,10 @@
     active = gate * sigma
     hidden = active * up
     weight_grad = jnp.sum(back * hidden, axis=1, keepdims=True)
-    sc_ref[...] = hidden.astype(BF)
-    d_gate = (back * up * sigma * (1.0 + gate * (1.0 - sigma))).astype(BF)
-    d_up = (back * active).astype(BF)
+    sc_ref[...] = (weight * hidden).astype(BF)
+    d_back = weight * back
+    d_gate = (d_back * up * sigma * (1.0 + gate * (1.0 - sigma))).astype(BF)
+    d_up = (d_back * active).astype(BF)
     dg_ref[...] = d_gate
     du_ref[...] = d_up
     contrib = lax.dot_general(d_gate, wg_ref[...], last, preferred_element_type=F32)
@@ -289,11 +292,7 @@
         )
         out_ref[0:LANES, :] = part.astype(out_ref.dtype)
         value = back_ref[:, b, :, width:].astype(F32).reshape(SLOTS, LANES)
-        grads = [
-            jnp.sum(jnp.where(h, value, 0.0), axis=0, keepdims=True)
-            / meta[k : k + 1, 2 * LANES :]
-            for k, h in enumerate(hits)
-        ]
+        grads = [jnp.sum(jnp.where(h, value, 0.0), axis=0, keepdims=True) for h in hits]
         grads.append(jnp.zeros((META - topk, LANES), F32))
         grads = jnp.concatenate(grads, axis=0)
         grads = jnp.concatenate([grads, jnp.zeros((META, width - LANES), F32)], axis=1)

time: 320 us -> 322 us (level)
  no operation moved by 1% of the time
where the time goes in v2:
time: 322 us; the launch traced here: 321 us
  waiting for transfers between devices  149 us (46%)
  Pallas kernels  65.4 us (20%)
  starting transfers between devices  59.1 us (18%)
  blocking collectives  31.5 us (10%)
  other arithmetic  12.2 us (4%)
    ppermute x14, waiting for transfers between devices, z_shift(): return lax.ppermute(value, ('z', 'c'), pairs)  80.3 us
    all_to_all x5, starting transfers between devices, plane_exchange(): return lax.all_to_all(value, PLANE, split_axis=0, concat_axis=0, tiled=True)  39.5 us
    all_to_all x5, waiting for transfers between devices, plane_exchange(): return lax.all_to_all(value, PLANE, split_axis=0, concat_axis=0, tiled=True)  35.4 us
    ppermute x4, waiting for transfers between devices, swap(): return lax.ppermute(value, axis, [(0, 1), (1, 0)])  33.4 us
    all_to_all x1, blocking collectives, plane_exchange(): return lax.all_to_all(value, PLANE, split_axis=0, concat_axis=0, tiled=True)  31.5 us
    pallas_call x3, Pallas kernels, expert(): pl.pallas_call(functools.partial(expert_kernel, len(carried)), grid=(1,),...  27.1 us
    ppermute x14, starting transfers between devices, z_shift(): return lax.ppermute(value, ('z', 'c'), pairs)  14.6 us
    pallas_call x3, Pallas kernels, build(): pl.pallas_call(functools.partial(build_kernel, topk, count), in_specs=[SM...  12.9 us
  transfers between devices with their start and end apart: 23, of which 10 were waited for; matrix products, arithmetic and copies ran while one was open for 3% of the time, Pallas kernels for 20%

profile of v2, /device:TPU:1, one launch (start us, length us, event | category | flops | bytes accessed | tf_op | source)
XLA Modules:
  0.0 320.5 jit_solution(12150927114671435795)
XLA Ops:
  0.6 2.4 pack.1.refs_0_
  3.0 3.2 collective-permute-start.1
  6.2 3.9 %collective-permute-start = (bf16[264,2048]{1,0:T(8,128)(2,1)}, bf16[264,2048]{1,0:T(8,128)(2,1)}, u32[]{:S(2)}, u32[]{:S(2)}) collective-permute-start(bf16[264,2048]{1,0:T(8,128)(2,1)} %pack.1.refs_0_), channel_id=1, source_target_pairs={{0,8},{1,57},{8,16},{9,1},{16,24},{17,9},{24,32},{25,17},{32,40},{... | collective-permute-start | bytes 3244040 | tf_op jit(solution)/shard_map/ppermute | solution.py:40
  10.1 2.7 collective-permute-start.2
  12.8 9.7 %collective-permute-done.refs_1_.refs_3_ = bf16[264,2048]{1,0:T(8,128)(2,1)} collective-permute-done((bf16[264,2048]{1,0:T(8,128)(2,1)}, bf16[264,2048]{1,0:T(8,128)(2,1)}, u32[]{:S(2)}, u32[]{:S(2)}) %collective-permute-start) | collective-permute-done | bytes 1081376 | tf_op jit(solution)/shard_map/ppermute | solution.py:40
  22.5 3.6 %build.3 = bf16[16,2,8,4224]{3,2,1,0:T(8,128)(2,1)} custom-call(s32[1]{0:T(128)} %bitcast.z_ref, bf16[264,2048]{1,0:T(8,128)(2,1)} %pack.1.refs_0_, bf16[264,2048]{1,0:T(8,128)(2,1)} %collective-permute-done.refs_1_.refs_3_), custom_call_target="tpu_custom_call" | custom-call | tf_op jit(solution)/shard_map/build/pallas_call | solution.py:127
  26.1 8.3 %all-to-all-start = ((bf16[16,2,8,4224]{3,2,1,0:T(8,128)(2,1)}), bf16[16,2,8,4224]{3,2,1,0:T(8,128)(2,1)}, u32[]{:S(2)}, u32[]{:S(2)}) async-start(bf16[16,2,8,4224]{3,2,1,0:T(8,128)(2,1)} %build.3), calls=%async_computation | async-start | bytes 4325376 | tf_op jit(solution)/shard_map/all_to_all | solution.py:319
  34.4 1.9 collective-permute-start.3
  36.3 0.9 collective-permute-start.4
  37.2 11.8 %collective-permute-done.3.refs_1_ = bf16[264,2048]{1,0:T(8,128)(2,1)} collective-permute-done((bf16[264,2048]{1,0:T(8,128)(2,1)}, bf16[264,2048]{1,0:T(8,128)(2,1)}, u32[]{:S(2)}, u32[]{:S(2)}) %collective-permute-start.3) | collective-permute-done | bytes 1081376 | tf_op jit(solution)/shard_map/ppermute | solution.py:40
  49.0 11.6 %collective-permute-done.4.refs_2_ = bf16[264,2048]{1,0:T(8,128)(2,1)} collective-permute-done((bf16[264,2048]{1,0:T(8,128)(2,1)}, bf16[264,2048]{1,0:T(8,128)(2,1)}, u32[]{:S(2)}, u32[]{:S(2)}) %collective-permute-start.4) | collective-permute-done | bytes 1081376 | tf_op jit(solution)/shard_map/ppermute | solution.py:40
  60.6 4.7 %build.4 = bf16[16,3,8,4224]{3,2,1,0:T(8,128)(2,1)} custom-call(s32[1]{0:T(128)} %bitcast.z_ref, bf16[264,2048]{1,0:T(8,128)(2,1)} %collective-permute-done.2.refs_0_, bf16[264,2048]{1,0:T(8,128)(2,1)} %collective-permute-done.3.refs_1_, bf16[264,2048]{1,0:T(8,128)(2,1)} %collective-permute-done.4.refs_2_), custom_call_target="tpu_custom_call" | custom-call | tf_op jit(solution)/shard_map/build/pallas_call | solution.py:127
  65.2 9.3 %all-to-all-start.2 = ((bf16[16,3,8,4224]{3,2,1,0:T(8,128)(2,1)}), bf16[16,3,8,4224]{3,2,1,0:T(8,128)(2,1)}, u32[]{:S(2)}, u32[]{:S(2)}) async-start(bf16[16,3,8,4224]{3,2,1,0:T(8,128)(2,1)} %build.4), calls=%async_computation.2 | async-start | bytes 6488064 | tf_op jit(solution)/shard_map/all_to_all | solution.py:319
  74.5 0.7 collective-permute-start.5
  75.2 13.9 %collective-permute-done.5.refs_0_ = bf16[264,2048]{1,0:T(8,128)(2,1)S(1)} collective-permute-done((bf16[264,2048]{1,0:T(8,128)(2,1)}, bf16[264,2048]{1,0:T(8,128)(2,1)S(1)}, u32[]{:S(2)}, u32[]{:S(2)}) %collective-permute-start.5) | collective-permute-done | bytes 1081376 | tf_op jit(solution)/shard_map/ppermute | solution.py:40
  89.1 1.0 copy-done
  90.2 1.9 collective-permute-start.7
  92.1 12.5 %collective-permute-done.7.refs_2_ = bf16[264,2048]{1,0:T(8,128)(2,1)S(1)} collective-permute-done((bf16[264,2048]{1,0:T(8,128)(2,1)S(1)}, bf16[264,2048]{1,0:T(8,128)(2,1)S(1)}, u32[]{:S(2)}, u32[]{:S(2)}) %collective-permute-start.7) | collective-permute-done | bytes 1081376 | tf_op jit(solution)/shard_map/ppermute | solution.py:40
  104.6 1.0 copy-done.1
  105.5 10.6 %collective-permute-done.6.refs_1_ = bf16[264,2048]{1,0:T(8,128)(2,1)} collective-permute-done((bf16[264,2048]{1,0:T(8,128)(2,1)}, bf16[264,2048]{1,0:T(8,128)(2,1)}, u32[]{:S(2)}, u32[]{:S(2)}) %collective-permute-start.6) | collective-permute-done | bytes 1081376 | tf_op jit(solution)/shard_map/ppermute | solution.py:40
  116.1 4.7 %build.5 = bf16[16,3,8,4224]{3,2,1,0:T(8,128)(2,1)} custom-call(s32[1]{0:T(128)} %bitcast.z_ref, bf16[264,2048]{1,0:T(8,128)(2,1)} %copy-done, bf16[264,2048]{1,0:T(8,128)(2,1)} %collective-permute-done.6.refs_1_, bf16[264,2048]{1,0:T(8,128)(2,1)} %copy-done.1), custom_call_target="tpu_custom_call" | custom-call | tf_op jit(solution)/shard_map/build/pallas_call | solution.py:127
  120.8 11.3 %all-to-all-start.4 = ((bf16[16,3,8,4224]{3,2,1,0:T(8,128)(2,1)}), bf16[16,3,8,4224]{3,2,1,0:T(8,128)(2,1)}, u32[]{:S(2)}, u32[]{:S(2)}) async-start(bf16[16,3,8,4224]{3,2,1,0:T(8,128)(2,1)} %build.5), calls=%async_computation.4 | async-start | bytes 6488064 | tf_op jit(solution)/shard_map/all_to_all | solution.py:319
  132.1 7.8 %expert.3 = (bf16[16,1,8,2176]{3,2,1,0:T(8,128)(2,1)}, bf16[16,4,8,2176]{3,2,1,0:T(8,128)(2,1)}, bf16[1024,4096]{1,0:T(8,128)(2,1)}, bf16[1024,384]{1,0:T(8,128)...) custom-call(bf16[256,4224]{1,0:T(8,128)(2,1)} %bitcast.3.rows_ref, bf16[2048,384]{1,0:T(8,128)(2,1)} %bitcast.18, ...), custom_call_target="tpu_custom_call" | custom-call | tf_op jit(solution)/shard_map/expert/pallas_call | solution.py:183
  139.9 35.4 %all-to-all-done.4 = bf16[16,3,8,4224]{3,2,1,0:T(8,128)(2,1)} async-done(((bf16[16,3,8,4224]{3,2,1,0:T(8,128)(2,1)}), bf16[16,3,8,4224]{3,2,1,0:T(8,128)(2,1)}, u32[]{:S(2)}, u32[]{:S(2)}) %all-to-all-start.4) | async-done | bytes 3244064 | tf_op jit(solution)/shard_map/all_to_all | solution.py:319
  175.3 6.1 %all-to-all-start.1 = ((bf16[16,1,8,2176]{3,2,1,0:T(8,128)(2,1)}), bf16[16,1,8,2176]{3,2,1,0:T(8,128)(2,1)S(1)}, u32[]{:S(2)}, u32[]{:S(2)}) async-start(bf16[16,1,8,2176]{3,2,1,0:T(8,128)(2,1)} %get-tuple-element.34), calls=%async_computation.1 | async-start | bytes 1114112 | tf_op jit(solution)/shard_map/all_to_all | solution.py:319
  181.4 10.3 %expert.4 = (bf16[16,4,8,2176]{3,2,1,0:T(8,128)(2,1)}, bf16[1024,4096]{1,0:T(8,128)(2,1)}, bf16[1024,384]{1,0:T(8,128)(2,1)}, bf16[1024,384]{1,0:T(8,128)(2,1)}, bf16[1024,384]{1,0:T(8,128)(2,1)}) custom-call(bf16[384,4224]{1,0:T(8,128)(2,1)} %bitcast.7.rows_ref, ...), custom_call_target="tpu_custom_call", output_to_operand_aliasing={{0}: (4, {}), {1}: (5, {}), {2}: (6, {}), {3}: (7, {}), {4}... | custom-call | tf_op jit(solution)/shard_map/expert/pallas_call | solution.py:183
  191.7 9.0 %expert.5 = (bf16[16,3,8,2176]{3,2,1,0:T(8,128)(2,1)}, bf16[1024,4096]{1,0:T(8,128)(2,1)}, bf16[1024,384]{1,0:T(8,128)(2,1)}, bf16[1024,384]{1,0:T(8,128)(2,1)}, bf16[1024,384]{1,0:T(8,128)(2,1)}) custom-call(bf16[384,4224]{1,0:T(8,128)(2,1)} %bitcast.8.rows_ref, ...), custom_call_target="tpu_custom_call", output_to_operand_aliasing={{1}: (4, {}), {2}: (5, {}), {3}: (6, {}), {4}: (7, {})} | custom-call | tf_op jit(solution)/shard_map/expert/pallas_call | solution.py:183
  200.7 31.5 %all_to_all.30.back_ref = bf16[16,3,8,2176]{3,2,1,0:T(8,128)(2,1)} all-to-all(bf16[16,3,8,2176]{3,2,1,0:T(8,128)(2,1)} %get-tuple-element.47), channel_id=1, replica_groups=mesh['rep'=2,'yh'=2,'z'=8,'x'=4,'c'=2] {'yh','x','c'}, dimensions={0} | all-to-all | bytes 3342336 | tf_op jit(solution)/shard_map/all_to_all | solution.py:319
  232.2 4.6 %all-to-all-start.3 = ((bf16[16,4,8,2176]{3,2,1,0:T(8,128)(2,1)}), bf16[16,4,8,2176]{3,2,1,0:T(8,128)(2,1)}, u32[]{:S(2)}, u32[]{:S(2)}) async-start(bf16[16,4,8,2176]{3,2,1,0:T(8,128)(2,1)} %get-tuple-element.40), calls=%async_computation.3 | async-start | bytes 4456448 | tf_op jit(solution)/shard_map/all_to_all | solution.py:319
  236.7 3.1 combine.5
  239.8 10.2 %collective-permute-done.8 = bf16[136,2048]{1,0:T(8,128)(2,1)S(1)} collective-permute-done((bf16[136,2048]{1,0:T(8,128)(2,1)}, bf16[136,2048]{1,0:T(8,128)(2,1)S(1)}, u32[]{:S(2)}, u32[]{:S(2)}) %collective-permute-start.8) | collective-permute-done | bytes 557088 | tf_op jit(solution)/shard_map/ppermute | solution.py:40
  250.0 2.0 add_convert_fusion.7
  252.0 2.4 combine.3
  254.5 5.6 %weights_down.1 = (bf16[192,2048]{1,0:T(8,128)(2,1)}, bf16[192,2048]{1,0:T(8,128)(2,1)}) custom-call(s32[1]{0:T(128)} %bitcast.10.rep_ref, bf16[1024,4096]{1,0:T(8,128)(2,1)} %get-tuple-element.53.x_ref.g_ref, bf16[1024,384]{1,0:T(8,128)(2,1)} %get-tuple-element.60.sc_ref), custom_call_target="tpu_custom_call" | custom-call | tf_op jit(solution)/shard_map/weights_down/pallas_call | solution.py:235
  260.5 8.5 %weights_gate_up.1 = (bf16[1024,384]{1,0:T(8,128)(2,1)}, bf16[1024,384]{1,0:T(8,128)(2,1)}, bf16[1024,384]{1,0:T(8,128)(2,1)}, bf16[1024,384]{1,0:T(8,128)(2,1)}) custom-call(s32[1]{0:T(128)} %bitcast.10.rep_ref, bf16[1024,4096]{1,0:T(8,128)(2,1)} %get-tuple-element.53.x_ref.g_ref, bf16[1024,384]{1,0:T(8,128)(2,1)} %get-tuple-element.54.dg_ref, ...), custom_call_target="tpu_custom_call" | custom-call | tf_op jit(solution)/shard_map/weights_gate_up/pallas_call | solution.py:262
  269.0 1.1 collective-permute-start.16
  270.4 3.4 %combine.4 = (bf16[136,2048]{1,0:T(8,128)(2,1)}, bf16[136,2048]{1,0:T(8,128)(2,1)}, bf16[136,2048]{1,0:T(8,128)(2,1)}, bf16[136,2048]{1,0:T(8,128)(2,1)}) custom-call(s32[1]{0:T(128)} %bitcast.z_ref, bf16[16,4,8,2176]{3,2,1,0:T(8,128)(2,1)} %all-to-all-done.3.back_ref, bf16[264,2048]{1,0:T(8,128)(2,1)} %collective-permute-done.2.refs_0_, ...), custom_call_target="tpu_custom_call" | custom-call | tf_op jit(solution)/shard_map/combine/pallas_call | solution.py:306
  273.9 1.4 add_convert_fusion.4
  275.4 1.3 add_convert_fusion.6
  276.7 1.7 collective-permute-start.10
  278.4 20.1 %collective-permute-done.16 = bf16[1024,384]{1,0:T(8,128)(2,1)} collective-permute-done((bf16[1024,384]{1,0:T(8,128)(2,1)}, bf16[1024,384]{1,0:T(8,128)(2,1)}, u32[]{:S(2)}, u32[]{:S(2)}) %collective-permute-start.16) | collective-permute-done | bytes 786464 | tf_op jit(solution)/shard_map/ppermute | solution.py:44
  298.5 2.3 fusion.3
  300.9 0.7 collective-permute-start.14
  302.1 13.3 %collective-permute-done.15 = bf16[1024,384]{1,0:T(8,128)(2,1)} collective-permute-done((bf16[1024,384]{1,0:T(8,128)(2,1)}, bf16[1024,384]{1,0:T(8,128)(2,1)}, u32[]{:S(2)}, u32[]{:S(2)}) %collective-permute-start.15) | collective-permute-done | bytes 786464 | tf_op jit(solution)/shard_map/ppermute | solution.py:44
  315.3 2.3 fusion.2
  317.6 1.2 fusion.4
  319.0 0.6 fusion.7
  319.5 1.0 fusion.1
  (41 shorter events, 1.7 us)
Async XLA Ops:
  3.0 7.1 %collective-permute-start.1 = (bf16[264,2048]{1,0:T(8,128)(2,1)}, bf16[264,2048]{1,0:T(8,128)(2,1)}, u32[]{:S(2)}, u32[]{:S(2)}) collective-permute-start(bf16[264,2048]{1,0:T(8,128)(2,1)} %pack.1.refs_0_), channel_id=1, source_target_pairs={{0,1},{1,0},{2,3},{3,2},{4,5},{5,4},{6,7},{7,6},{8,9},{9,8},{10,11... | collective-permute-start | bytes 3244040 | tf_op jit(solution)/shard_map/ppermute | solution.py:44
  6.2 16.3 %collective-permute-start = (bf16[264,2048]{1,0:T(8,128)(2,1)}, bf16[264,2048]{1,0:T(8,128)(2,1)}, u32[]{:S(2)}, u32[]{:S(2)}) collective-permute-start(bf16[264,2048]{1,0:T(8,128)(2,1)} %pack.1.refs_0_), channel_id=1, source_target_pairs={{0,8},{1,57},{8,16},{9,1},{16,24},{17,9},{24,32},{25,17},{32,40},{... | collective-permute-start | bytes 3244040 | tf_op jit(solution)/shard_map/ppermute | solution.py:40
  10.1 26.2 %collective-permute-start.2 = (bf16[264,2048]{1,0:T(8,128)(2,1)}, bf16[264,2048]{1,0:T(8,128)(2,1)}, u32[]{:S(2)}, u32[]{:S(2)}) collective-permute-start(bf16[264,2048]{1,0:T(8,128)(2,1)} %collective-permute-done.1), channel_id=1, source_target_pairs={{0,8},{1,57},{8,16},{9,1},{16,24},{17,9},{24,32},{25,17},{32,40},{... | collective-permute-start | bytes 3244040 | tf_op jit(solution)/shard_map/ppermute | solution.py:40
  26.1 39.1 %all-to-all-start = ((bf16[16,2,8,4224]{3,2,1,0:T(8,128)(2,1)}), bf16[16,2,8,4224]{3,2,1,0:T(8,128)(2,1)}, u32[]{:S(2)}, u32[]{:S(2)}) async-start(bf16[16,2,8,4224]{3,2,1,0:T(8,128)(2,1)} %build.3), calls=%async_computation | async-start | bytes 4325376 | tf_op jit(solution)/shard_map/all_to_all | solution.py:319
  34.4 14.6 %collective-permute-start.3 = (bf16[264,2048]{1,0:T(8,128)(2,1)}, bf16[264,2048]{1,0:T(8,128)(2,1)}, u32[]{:S(2)}, u32[]{:S(2)}) collective-permute-start(bf16[264,2048]{1,0:T(8,128)(2,1)} %collective-permute-done.refs_1_.refs_3_), channel_id=1, source_target_pairs={{0,8},{1,57},{8,16},{9,1},{16,24},{17,9},{24,32},{25,17},{32,40},{... | collective-permute-start | bytes 3244040 | tf_op jit(solution)/shard_map/ppermute | solution.py:40
  36.3 24.3 %collective-permute-start.4 = (bf16[264,2048]{1,0:T(8,128)(2,1)}, bf16[264,2048]{1,0:T(8,128)(2,1)}, u32[]{:S(2)}, u32[]{:S(2)}) collective-permute-start(bf16[264,2048]{1,0:T(8,128)(2,1)} %collective-permute-done.2.refs_0_), channel_id=1, source_target_pairs={{0,8},{1,57},{8,16},{9,1},{16,24},{17,9},{24,32},{25,17},{32,40},{... | collective-permute-start | bytes 3244040 | tf_op jit(solution)/shard_map/ppermute | solution.py:40
  65.2 55.6 %all-to-all-start.2 = ((bf16[16,3,8,4224]{3,2,1,0:T(8,128)(2,1)}), bf16[16,3,8,4224]{3,2,1,0:T(8,128)(2,1)}, u32[]{:S(2)}, u32[]{:S(2)}) async-start(bf16[16,3,8,4224]{3,2,1,0:T(8,128)(2,1)} %build.4), calls=%async_computation.2 | async-start | bytes 6488064 | tf_op jit(solution)/shard_map/all_to_all | solution.py:319
  74.5 14.6 %collective-permute-start.5 = (bf16[264,2048]{1,0:T(8,128)(2,1)}, bf16[264,2048]{1,0:T(8,128)(2,1)S(1)}, u32[]{:S(2)}, u32[]{:S(2)}) collective-permute-start(bf16[264,2048]{1,0:T(8,128)(2,1)} %collective-permute-done.3.refs_1_), channel_id=1, source_target_pairs={{0,8},{1,57},{8,16},{9,1},{16,24},{17,9},{24,32},{25,17},{32,40},{... | collective-permute-start | bytes 3244040 | tf_op jit(solution)/shard_map/ppermute | solution.py:40
  89.1 1.0 copy-start
  90.2 14.4 %collective-permute-start.7 = (bf16[264,2048]{1,0:T(8,128)(2,1)S(1)}, bf16[264,2048]{1,0:T(8,128)(2,1)S(1)}, u32[]{:S(2)}, u32[]{:S(2)}) collective-permute-start(bf16[264,2048]{1,0:T(8,128)(2,1)S(1)} %collective-permute-done.5.refs_0_), channel_id=1, source_target_pairs={{0,8},{1,57},{8,16},{9,1},{16,24},{17,9},{24,32},{25,17},{32,40},{... | collective-permute-start | bytes 3244040 | tf_op jit(solution)/shard_map/ppermute | solution.py:40
  92.1 24.1 %collective-permute-start.6 = (bf16[264,2048]{1,0:T(8,128)(2,1)}, bf16[264,2048]{1,0:T(8,128)(2,1)}, u32[]{:S(2)}, u32[]{:S(2)}) collective-permute-start(bf16[264,2048]{1,0:T(8,128)(2,1)} %collective-permute-done.4.refs_2_), channel_id=1, source_target_pairs={{0,8},{1,57},{8,16},{9,1},{16,24},{17,9},{24,32},{25,17},{32,40},{... | collective-permute-start | bytes 3244040 | tf_op jit(solution)/shard_map/ppermute | solution.py:40
  104.6 1.0 copy-start.1
  120.8 54.5 %all-to-all-start.4 = ((bf16[16,3,8,4224]{3,2,1,0:T(8,128)(2,1)}), bf16[16,3,8,4224]{3,2,1,0:T(8,128)(2,1)}, u32[]{:S(2)}, u32[]{:S(2)}) async-start(bf16[16,3,8,4224]{3,2,1,0:T(8,128)(2,1)} %build.5), calls=%async_computation.4 | async-start | bytes 6488064 | tf_op jit(solution)/shard_map/all_to_all | solution.py:319
  175.3 25.4 %all-to-all-start.1 = ((bf16[16,1,8,2176]{3,2,1,0:T(8,128)(2,1)}), bf16[16,1,8,2176]{3,2,1,0:T(8,128)(2,1)S(1)}, u32[]{:S(2)}, u32[]{:S(2)}) async-start(bf16[16,1,8,2176]{3,2,1,0:T(8,128)(2,1)} %get-tuple-element.34), calls=%async_computation.1 | async-start | bytes 1114112 | tf_op jit(solution)/shard_map/all_to_all | solution.py:319
  200.7 31.5 %copy-start.3 = (bf16[16,1,8,2176]{3,2,1,0:T(8,128)(2,1)}, bf16[16,1,8,2176]{3,2,1,0:T(8,128)(2,1)S(1)}, u32[]{:S(2)}) copy-start(bf16[16,1,8,2176]{3,2,1,0:T(8,128)(2,1)S(1)} %all-to-all-done.1.back_ref) | copy-start | bytes 1671172
  232.2 38.3 %all-to-all-start.3 = ((bf16[16,4,8,2176]{3,2,1,0:T(8,128)(2,1)}), bf16[16,4,8,2176]{3,2,1,0:T(8,128)(2,1)}, u32[]{:S(2)}, u32[]{:S(2)}) async-start(bf16[16,4,8,2176]{3,2,1,0:T(8,128)(2,1)} %get-tuple-element.40), calls=%async_computation.3 | async-start | bytes 4456448 | tf_op jit(solution)/shard_map/all_to_all | solution.py:319
  239.8 10.2 %collective-permute-start.8 = (bf16[136,2048]{1,0:T(8,128)(2,1)}, bf16[136,2048]{1,0:T(8,128)(2,1)S(1)}, u32[]{:S(2)}, u32[]{:S(2)}) collective-permute-start(bf16[136,2048]{1,0:T(8,128)(2,1)} %get-tuple-element.49), channel_id=1, source_target_pairs={{0,56},{1,9},{8,0},{9,17},{16,8},{17,25},{24,16},{25,33},{32,24},{... | collective-permute-start | bytes 1671176 | tf_op jit(solution)/shard_map/ppermute | solution.py:40
  239.8 34.1 %collective-permute-start.12 = (bf16[136,2048]{1,0:T(8,128)(2,1)}, bf16[136,2048]{1,0:T(8,128)(2,1)}, u32[]{:S(2)}, u32[]{:S(2)}) collective-permute-start(bf16[136,2048]{1,0:T(8,128)(2,1)} %get-tuple-element.52), channel_id=1, source_target_pairs={{0,56},{1,9},{8,0},{9,17},{16,8},{17,25},{24,16},{25,33},{32,24},{... | collective-permute-start | bytes 1671176 | tf_op jit(solution)/shard_map/ppermute | solution.py:40
  252.0 23.4 %collective-permute-start.9 = (bf16[136,2048]{1,0:T(8,128)(2,1)}, bf16[136,2048]{1,0:T(8,128)(2,1)}, u32[]{:S(2)}, u32[]{:S(2)}) collective-permute-start(bf16[136,2048]{1,0:T(8,128)(2,1)} %add_convert_fusion.7), channel_id=1, source_target_pairs={{0,56},{1,9},{8,0},{9,17},{16,8},{17,25},{24,16},{25,33},{32,24},{... | collective-permute-start | bytes 1671176 | tf_op jit(solution)/shard_map/ppermute | solution.py:40
  260.1 57.6 %collective-permute-start.17 = (bf16[192,2048]{1,0:T(8,128)(2,1)}, bf16[192,2048]{1,0:T(8,128)(2,1)S(1)}, u32[]{:S(2)}, u32[]{:S(2)}) collective-permute-start(bf16[192,2048]{1,0:T(8,128)(2,1)} %get-tuple-element.62), channel_id=1, source_target_pairs={{0,128},{128,0},{1,129},{129,1},{2,130},{130,2},{3,131},{131,3},{4... | collective-permute-start | bytes 2359304 | tf_op jit(solution)/shard_map/ppermute | solution.py:44
  269.0 29.5 %collective-permute-start.16 = (bf16[1024,384]{1,0:T(8,128)(2,1)}, bf16[1024,384]{1,0:T(8,128)(2,1)}, u32[]{:S(2)}, u32[]{:S(2)}) collective-permute-start(bf16[1024,384]{1,0:T(8,128)(2,1)} %get-tuple-element.59), channel_id=1, source_target_pairs={{0,128},{128,0},{1,129},{129,1},{2,130},{130,2},{3,131},{131,3},{4... | collective-permute-start | bytes 2359304 | tf_op jit(solution)/shard_map/ppermute | solution.py:44
  270.0 45.3 %collective-permute-start.15 = (bf16[1024,384]{1,0:T(8,128)(2,1)}, bf16[1024,384]{1,0:T(8,128)(2,1)}, u32[]{:S(2)}, u32[]{:S(2)}) collective-permute-start(bf16[1024,384]{1,0:T(8,128)(2,1)} %get-tuple-element.57), channel_id=1, source_target_pairs={{0,128},{128,0},{1,129},{129,1},{2,130},{130,2},{3,131},{131,3},{4... | collective-permute-start | bytes 2359304 | tf_op jit(solution)/shard_map/ppermute | solution.py:44
  273.9 1.5 copy-start.9
  275.3 23.2 %copy-start.6 = (bf16[1024,384]{1,0:T(8,128)(2,1)S(1)}, bf16[1024,384]{1,0:T(8,128)(2,1)}, u32[]{:S(2)}) copy-start(bf16[1024,384]{1,0:T(8,128)(2,1)} %get-tuple-element.58) | copy-start | bytes 2359300
  275.3 25.5 %collective-permute-start.13 = (bf16[136,2048]{1,0:T(8,128)(2,1)S(1)}, bf16[136,2048]{1,0:T(8,128)(2,1)S(1)}, u32[]{:S(2)}, u32[]{:S(2)}) collective-permute-start(bf16[136,2048]{1,0:T(8,128)(2,1)S(1)} %add_convert_fusion.4), channel_id=1, source_target_pairs={{0,56},{1,9},{8,0},{9,17},{16,8},{17,25},{24,16},{25,33},{32,24},{... | collective-permute-start | bytes 1671176 | tf_op jit(solution)/shard_map/ppermute | solution.py:40
  276.7 24.9 %collective-permute-start.10 = (bf16[136,2048]{1,0:T(8,128)(2,1)S(1)}, bf16[136,2048]{1,0:T(8,128)(2,1)S(1)}, u32[]{:S(2)}, u32[]{:S(2)}) collective-permute-start(bf16[136,2048]{1,0:T(8,128)(2,1)S(1)} %add_convert_fusion.6), channel_id=1, source_target_pairs={{0,56},{1,9},{8,0},{9,17},{16,8},{17,25},{24,16},{25,33},{32,24},{... | collective-permute-start | bytes 1671176 | tf_op jit(solution)/shard_map/ppermute | solution.py:40
  298.5 2.3 copy-start.8
  300.8 1.1 copy-start.7
  300.9 14.4 %copy-start.5 = (bf16[1024,384]{1,0:T(8,128)(2,1)S(1)}, bf16[1024,384]{1,0:T(8,128)(2,1)}, u32[]{:S(2)}) copy-start(bf16[1024,384]{1,0:T(8,128)(2,1)} %get-tuple-element.56) | copy-start | bytes 2359300
  300.9 17.9 %collective-permute-start.14 = (bf16[136,2048]{1,0:T(8,128)(2,1)S(1)}, bf16[136,2048]{1,0:T(8,128)(2,1)S(1)}, u32[]{:S(2)}, u32[]{:S(2)}) collective-permute-start(bf16[136,2048]{1,0:T(8,128)(2,1)S(1)} %add_convert_fusion.3), channel_id=1, source_target_pairs={{0,57},{1,8},{8,1},{9,16},{16,9},{17,24},{24,17},{25,32},{32,25},{... | collective-permute-start | bytes 1671176 | tf_op jit(solution)/shard_map/ppermute | solution.py:40
  302.0 16.8 %collective-permute-start.11 = (bf16[136,2048]{1,0:T(8,128)(2,1)S(1)}, bf16[136,2048]{1,0:T(8,128)(2,1)S(1)}, u32[]{:S(2)}, u32[]{:S(2)}) collective-permute-start(bf16[136,2048]{1,0:T(8,128)(2,1)S(1)} %add_convert_fusion.5), channel_id=1, source_target_pairs={{0,56},{1,9},{8,0},{9,17},{16,8},{17,25},{24,16},{25,33},{32,24},{... | collective-permute-start | bytes 1671176 | tf_op jit(solution)/shard_map/ppermute | solution.py:40
  315.3 2.3 copy-start.4
  317.6 1.3 copy-start.2
